TPU v7x, 256 devices: a whole 4x4x8 slice. The times are simulated.
256 devices in a mesh: clique: 8 (over y_hi, x), copy: 32 (over z, y_lo, core).
Axes of the slice: x: 4, y: 4 (y_hi: 2, y_lo: 2; y = y_hi * 2 + y_lo), z: 8, core: 2. Of those that a mesh axis runs over, the one named last changes fastest.
Arguments:
- out_grad: bfloat16 [524288, 512], P(('clique', 'copy')), may hold values from -6 to 6
- pre_act: bfloat16 [524288, 512], P(('clique', 'copy')), may hold values from -6 to 6
- batch_count: int32 [256], P(('clique', 'copy')), may hold values from 1024 to 2048, as said below
- layer_two: bfloat16 [512, 512], replicated, may hold values from -0.25 to 0.25
- hot_slots: int32 [524288, 10], P(('clique', 'copy')), may hold values from 0 to 4095
- cold_index: int32 [524288, 15], P(('clique', 'copy')), may hold values from 0 to 2047
- hot_feats: bfloat16 [4096, 768], P('clique'), may hold values from -6 to 6
- cold_feats: bfloat16 [524288, 768], P(('clique', 'copy')), may hold values from -6 to 6
Outputs:
- grad_one: float32 [768, 512], replicated
- grad_two: float32 [512, 512], replicated
Inputs may be any that keep to these rules, and one draw needn't show every extreme that they name: `batch_count`: some device has all 2048 rows live in every draw.
All inputs are finite; a program needn't handle non-finite values.
Results may differ from a plain program's by a relative error of at most 0.015.
Values may be sent and summed in bfloat16 or wider, within the bound.
A program may use at most 128 MiB of HBM per device.

v0:
```python
import jax
import jax.numpy as jnp
from jax import lax
from jax.sharding import PartitionSpec as P


def table_sums(index_cols, row_grad, table_rows, fanout):
    block = min(512, table_rows)
    blocks = table_rows // block
    offsets = jnp.arange(block, dtype=jnp.int32)

    def one_block(start):
        wanted = start + offsets
        counts = jnp.zeros((block, index_cols.shape[0]), jnp.float32)
        for column in range(index_cols.shape[1]):
            counts = counts + (index_cols[:, column][None, :] == wanted[:, None]).astype(
                jnp.float32
            )
        summed = jnp.dot(counts.astype(jnp.bfloat16), row_grad, preferred_element_type=jnp.float32)
        return (summed * (1.0 / fanout)).astype(jnp.bfloat16)

    starts = jnp.arange(blocks, dtype=jnp.int32) * block
    parts = lax.map(one_block, starts)
    return parts.reshape(table_rows, row_grad.shape[1])


def on_device(
    out_grad, pre_act, batch_count, layer_two, hot_slots, cold_index, hot_feats, cold_feats
):
    rows = out_grad.shape[0]
    hot_local = hot_feats.shape[0]
    hot_total = hot_local * lax.axis_size("clique")
    k_hot = hot_slots.shape[1]
    k_cold = cold_index.shape[1]
    fanout = k_hot + k_cold
    cold_rows = cold_feats.shape[0]
    live = (jnp.arange(rows, dtype=jnp.int32) < batch_count[0])[:, None]
    masked = jnp.where(live, out_grad, jnp.zeros_like(out_grad))
    activ = jnp.maximum(pre_act, jnp.zeros_like(pre_act))
    grad_two = jnp.dot(activ.T, masked, preferred_element_type=jnp.float32)
    back = jnp.dot(masked, layer_two.T, preferred_element_type=jnp.float32)
    row_grad = jnp.where(pre_act > 0, back, jnp.zeros_like(back)).astype(jnp.bfloat16)
    hot_part = table_sums(hot_slots, row_grad, hot_total, fanout)
    summed = lax.psum(hot_part, "clique").astype(jnp.float32)
    owned = lax.dynamic_slice_in_dim(summed, lax.axis_index("clique") * hot_local, hot_local, 0)
    cold_part = table_sums(cold_index, row_grad, cold_rows, fanout)
    grad_one = jnp.dot(cold_feats.T, cold_part, preferred_element_type=jnp.float32)
    grad_one = grad_one + jnp.dot(
        hot_feats.T, owned.astype(jnp.bfloat16), preferred_element_type=jnp.float32
    )
    total_one, total_two = lax.psum((grad_one, grad_two), ("clique", "copy"))
    return (total_one, total_two)


def solution(mesh):
    placed = (
        P(("clique", "copy"), None),
        P(("clique", "copy"), None),
        P(("clique", "copy")),
        P(),
        P(("clique", "copy"), None),
        P(("clique", "copy"), None),
        P("clique", None),
        P(("clique", "copy"), None),
    )
    return jax.shard_map(
        on_device, mesh=mesh, in_specs=placed, out_specs=(P(), P()), check_vma=False
    )
```

profile of v0, /device:TPU:1, one launch (start us, length us, event | category | flops | bytes accessed | tf_op | source)
XLA Modules:
  0.0 474.2 jit_solution(12058573302038147682)
XLA Ops:
  8.1 5.2 %select_convert_fusion = bf16[2048,512]{1,0:T(8,128)(2,1)} fusion(bf16[2048,512]{1,0:T(8,128)(2,1)} %param.13, bf16[512,512]{1,0:T(8,128)(2,1)} %param.15, bf16[2048,512]{1,0:T(8,128)(2,1)} %param.12, pred[2048]{0:T(1024)(128)(4,1)S(1)} %iota_compare_fusion), kind=kOutput, calls=%fused_computation.43 | convolution fusion | flops 1077936128 | bytes 6817792 | tf_op jit(solution)/shard_map/dot_general | solution.py:41
  13.2 63.4 %while.23 = (s32[]{:T(128)}, bf16[8,512,512]{2,1,0:T(8,128)(2,1)}, s32[2048,10]{0,1:T(8,128)S(1)}, s32[8]{0:T(128)S(1)}, bf16[2048,512]{1,0:T(8,128)(2,1)}, /*index=5*/s32[]{:T(128)}) while((s32[]{:T(128)}, bf16[8,512,512]{2,1,0:T(8,128)(2,1)}, s32[2048,10]{0,1:T(8,128)S(1)}, s32[8]{0:T(128)S(1)}, bf16[2048,512]{1,0:T(8,128)(2,1)}, ...), condition=%wide.region_3.4_spmd.clone, body=%wide.region_2.3_spmd.clone.sunk | while | flops 1105723904 | bytes 2871893 | solution.py:23
  13.3 0.6 dynamic_slice.22
  13.9 0.6 iota_add_fusion.5
  14.6 6.6 %fusion.68 = bf16[8,512,512]{2,1,0:T(8,128)(2,1)} fusion(bf16[8,512,512]{2,1,0:T(8,128)(2,1)} %get-tuple-element.278, s32[]{:T(128)} %get-tuple-element.277, bf16[2048,512]{1,0:T(8,128)(2,1)} %get-tuple-element.287, s32[2048]{0:T(1024)S(1)} %bitcast.126, s32[2048]{0:T(1024)S(1)} %bitcast.127, s32[2048]{0:T(1024)S(1)} %bitcast.128, ...), kind=kOutput, calls=%fused_computation.41.clone.1 | convolution fusion | flops 1105723392 | bytes 2705920 | tf_op jit(solution)/shard_map/while/body/eval_jaxpr/dot_general | solution.py:19
  21.2 0.6 dynamic_slice.22
  21.9 0.6 iota_add_fusion.5
  22.5 6.6 %fusion.68 = bf16[8,512,512]{2,1,0:T(8,128)(2,1)} fusion(bf16[8,512,512]{2,1,0:T(8,128)(2,1)} %get-tuple-element.278, s32[]{:T(128)} %get-tuple-element.277, bf16[2048,512]{1,0:T(8,128)(2,1)} %get-tuple-element.287, s32[2048]{0:T(1024)S(1)} %bitcast.126, s32[2048]{0:T(1024)S(1)} %bitcast.127, s32[2048]{0:T(1024)S(1)} %bitcast.128, ...), kind=kOutput, calls=%fused_computation.41.clone.1 | convolution fusion | flops 1105723392 | bytes 2705920 | tf_op jit(solution)/shard_map/while/body/eval_jaxpr/dot_general | solution.py:19
  29.2 0.6 dynamic_slice.22
  29.8 0.6 iota_add_fusion.5
  30.4 6.6 %fusion.68 = bf16[8,512,512]{2,1,0:T(8,128)(2,1)} fusion(bf16[8,512,512]{2,1,0:T(8,128)(2,1)} %get-tuple-element.278, s32[]{:T(128)} %get-tuple-element.277, bf16[2048,512]{1,0:T(8,128)(2,1)} %get-tuple-element.287, s32[2048]{0:T(1024)S(1)} %bitcast.126, s32[2048]{0:T(1024)S(1)} %bitcast.127, s32[2048]{0:T(1024)S(1)} %bitcast.128, ...), kind=kOutput, calls=%fused_computation.41.clone.1 | convolution fusion | flops 1105723392 | bytes 2705920 | tf_op jit(solution)/shard_map/while/body/eval_jaxpr/dot_general | solution.py:19
  37.1 0.6 dynamic_slice.22
  37.7 0.6 iota_add_fusion.5
  38.4 6.6 %fusion.68 = bf16[8,512,512]{2,1,0:T(8,128)(2,1)} fusion(bf16[8,512,512]{2,1,0:T(8,128)(2,1)} %get-tuple-element.278, s32[]{:T(128)} %get-tuple-element.277, bf16[2048,512]{1,0:T(8,128)(2,1)} %get-tuple-element.287, s32[2048]{0:T(1024)S(1)} %bitcast.126, s32[2048]{0:T(1024)S(1)} %bitcast.127, s32[2048]{0:T(1024)S(1)} %bitcast.128, ...), kind=kOutput, calls=%fused_computation.41.clone.1 | convolution fusion | flops 1105723392 | bytes 2705920 | tf_op jit(solution)/shard_map/while/body/eval_jaxpr/dot_general | solution.py:19
  45.0 0.6 dynamic_slice.22
  45.6 0.6 iota_add_fusion.5
  46.3 6.6 %fusion.68 = bf16[8,512,512]{2,1,0:T(8,128)(2,1)} fusion(bf16[8,512,512]{2,1,0:T(8,128)(2,1)} %get-tuple-element.278, s32[]{:T(128)} %get-tuple-element.277, bf16[2048,512]{1,0:T(8,128)(2,1)} %get-tuple-element.287, s32[2048]{0:T(1024)S(1)} %bitcast.126, s32[2048]{0:T(1024)S(1)} %bitcast.127, s32[2048]{0:T(1024)S(1)} %bitcast.128, ...), kind=kOutput, calls=%fused_computation.41.clone.1 | convolution fusion | flops 1105723392 | bytes 2705920 | tf_op jit(solution)/shard_map/while/body/eval_jaxpr/dot_general | solution.py:19
  52.9 0.6 dynamic_slice.22
  53.6 0.6 iota_add_fusion.5
  54.2 6.6 %fusion.68 = bf16[8,512,512]{2,1,0:T(8,128)(2,1)} fusion(bf16[8,512,512]{2,1,0:T(8,128)(2,1)} %get-tuple-element.278, s32[]{:T(128)} %get-tuple-element.277, bf16[2048,512]{1,0:T(8,128)(2,1)} %get-tuple-element.287, s32[2048]{0:T(1024)S(1)} %bitcast.126, s32[2048]{0:T(1024)S(1)} %bitcast.127, s32[2048]{0:T(1024)S(1)} %bitcast.128, ...), kind=kOutput, calls=%fused_computation.41.clone.1 | convolution fusion | flops 1105723392 | bytes 2705920 | tf_op jit(solution)/shard_map/while/body/eval_jaxpr/dot_general | solution.py:19
  60.9 0.6 dynamic_slice.22
  61.5 0.6 iota_add_fusion.5
  62.1 6.6 %fusion.68 = bf16[8,512,512]{2,1,0:T(8,128)(2,1)} fusion(bf16[8,512,512]{2,1,0:T(8,128)(2,1)} %get-tuple-element.278, s32[]{:T(128)} %get-tuple-element.277, bf16[2048,512]{1,0:T(8,128)(2,1)} %get-tuple-element.287, s32[2048]{0:T(1024)S(1)} %bitcast.126, s32[2048]{0:T(1024)S(1)} %bitcast.127, s32[2048]{0:T(1024)S(1)} %bitcast.128, ...), kind=kOutput, calls=%fused_computation.41.clone.1 | convolution fusion | flops 1105723392 | bytes 2705920 | tf_op jit(solution)/shard_map/while/body/eval_jaxpr/dot_general | solution.py:19
  68.8 0.6 dynamic_slice.22
  69.4 0.6 iota_add_fusion.5
  70.1 6.6 %fusion.68 = bf16[8,512,512]{2,1,0:T(8,128)(2,1)} fusion(bf16[8,512,512]{2,1,0:T(8,128)(2,1)} %get-tuple-element.278, s32[]{:T(128)} %get-tuple-element.277, bf16[2048,512]{1,0:T(8,128)(2,1)} %get-tuple-element.287, s32[2048]{0:T(1024)S(1)} %bitcast.126, s32[2048]{0:T(1024)S(1)} %bitcast.127, s32[2048]{0:T(1024)S(1)} %bitcast.128, ...), kind=kOutput, calls=%fused_computation.41.clone.1 | convolution fusion | flops 1105723392 | bytes 2705920 | tf_op jit(solution)/shard_map/while/body/eval_jaxpr/dot_general | solution.py:19
  76.7 0.2 all-reduce.6.cloned.1.call-start
  77.0 4.6 fusion.41
  81.5 39.9 %while.22 = (s32[]{:T(128)}, bf16[4,512,512]{2,1,0:T(8,128)(2,1)}, s32[2048,15]{0,1:T(8,128)S(1)}, s32[4]{0:T(128)S(1)}, bf16[2048,512]{1,0:T(8,128)(2,1)}, /*index=5*/s32[]{:T(128)}) while((s32[]{:T(128)}, bf16[4,512,512]{2,1,0:T(8,128)(2,1)}, s32[2048,15]{0,1:T(8,128)S(1)}, s32[4]{0:T(128)S(1)}, bf16[2048,512]{1,0:T(8,128)(2,1)}, ...), condition=%wide.region_1.2_spmd.clone, body=%wide.region_0.1_spmd.clone.sunk | while | flops 1121452544 | bytes 2994773 | solution.py:23
  81.6 0.6 dynamic_slice.21
  82.2 0.6 iota_add_fusion.4
  82.9 8.6 %fusion.65 = bf16[4,512,512]{2,1,0:T(8,128)(2,1)} fusion(bf16[4,512,512]{2,1,0:T(8,128)(2,1)} %get-tuple-element.260, s32[]{:T(128)} %get-tuple-element.259, bf16[2048,512]{1,0:T(8,128)(2,1)} %get-tuple-element.269, s32[2048]{0:T(1024)S(1)} %bitcast.111, s32[2048]{0:T(1024)S(1)} %bitcast.112, s32[2048]{0:T(1024)S(1)} %bitcast.113, ...), kind=kOutput, calls=%fused_computation.23.clone.1 | convolution fusion | flops 1121452032 | bytes 2746880 | tf_op jit(solution)/shard_map/while/body/eval_jaxpr/dot_general | solution.py:19
  91.6 0.6 dynamic_slice.21
  92.2 0.6 iota_add_fusion.4
  92.9 8.6 %fusion.65 = bf16[4,512,512]{2,1,0:T(8,128)(2,1)} fusion(bf16[4,512,512]{2,1,0:T(8,128)(2,1)} %get-tuple-element.260, s32[]{:T(128)} %get-tuple-element.259, bf16[2048,512]{1,0:T(8,128)(2,1)} %get-tuple-element.269, s32[2048]{0:T(1024)S(1)} %bitcast.111, s32[2048]{0:T(1024)S(1)} %bitcast.112, s32[2048]{0:T(1024)S(1)} %bitcast.113, ...), kind=kOutput, calls=%fused_computation.23.clone.1 | convolution fusion | flops 1121452032 | bytes 2746880 | tf_op jit(solution)/shard_map/while/body/eval_jaxpr/dot_general | solution.py:19
  101.5 0.1 fusion.64
  101.5 0.6 dynamic_slice.21
  102.2 0.6 iota_add_fusion.4
  102.8 8.6 %fusion.65 = bf16[4,512,512]{2,1,0:T(8,128)(2,1)} fusion(bf16[4,512,512]{2,1,0:T(8,128)(2,1)} %get-tuple-element.260, s32[]{:T(128)} %get-tuple-element.259, bf16[2048,512]{1,0:T(8,128)(2,1)} %get-tuple-element.269, s32[2048]{0:T(1024)S(1)} %bitcast.111, s32[2048]{0:T(1024)S(1)} %bitcast.112, s32[2048]{0:T(1024)S(1)} %bitcast.113, ...), kind=kOutput, calls=%fused_computation.23.clone.1 | convolution fusion | flops 1121452032 | bytes 2746880 | tf_op jit(solution)/shard_map/while/body/eval_jaxpr/dot_general | solution.py:19
  111.5 0.6 dynamic_slice.21
  112.1 0.6 iota_add_fusion.4
  112.8 8.7 %fusion.65 = bf16[4,512,512]{2,1,0:T(8,128)(2,1)} fusion(bf16[4,512,512]{2,1,0:T(8,128)(2,1)} %get-tuple-element.260, s32[]{:T(128)} %get-tuple-element.259, bf16[2048,512]{1,0:T(8,128)(2,1)} %get-tuple-element.269, s32[2048]{0:T(1024)S(1)} %bitcast.111, s32[2048]{0:T(1024)S(1)} %bitcast.112, s32[2048]{0:T(1024)S(1)} %bitcast.113, ...), kind=kOutput, calls=%fused_computation.23.clone.1 | convolution fusion | flops 1121452032 | bytes 2746880 | tf_op jit(solution)/shard_map/while/body/eval_jaxpr/dot_general | solution.py:19
  121.4 4.6 fusion.50
  126.0 69.5 %all-reduce.4.cloned.1.call-done = bf16[4096,512]{1,0:T(8,128)(2,1)} async-done(((bf16[4096,512]{1,0:T(8,128)(2,1)}), bf16[4096,512]{1,0:T(8,128)(2,1)}) %all-reduce.4.cloned.1.call-update) | async-done | bytes 4194320 | tf_op jit(solution)/shard_map/psum | solution.py:44
  195.6 3.6 add_bitcast_fusion
  199.2 262.9 %all-reduce.6.cloned.1.call-done = (f32[768,512]{0,1:T(8,128)}, f32[512,512]{1,0:T(8,128)}) async-done(((f32[768,512]{0,1:T(8,128)}, f32[512,512]{1,0:T(8,128)}), (f32[768,512]{0,1:T(8,128)}, f32[512,512]{1,0:T(8,128)})) %all-reduce.6.cloned.1.call-update) | async-done | bytes 2621456 | tf_op jit(solution)/shard_map/psum | solution.py:51
  462.1 3.0 copy.10
  465.1 2.3 copy.30
  (25 shorter events, 0.8 us)
Async XLA Ops:
  7.2 114.3 %copy-start = (bf16[2048,768]{1,0:T(8,128)(2,1)S(1)}, bf16[2048,768]{1,0:T(8,128)(2,1)}, u32[]{:S(2)}) copy-start(bf16[2048,768]{1,0:T(8,128)(2,1)} %param.19) | copy-start | bytes 9437188
  7.2 188.4 %all-reduce.4.cloned.1.call-start = ((), (), s32[]{:S(2)}) async-start(), calls=%async_computation | async-start | bytes 8388608 | tf_op jit(solution)/shard_map/psum | solution.py:44
  8.1 5.2 %copy-start.2 = (s32[2048,10]{0,1:T(8,128)S(1)}, s32[2048,10]{0,1:T(8,128)}, u32[]{:S(2)}) copy-start(s32[2048,10]{0,1:T(8,128)} %param.16) | copy-start | bytes 245764
  76.7 4.8 %copy-start.1 = (s32[2048,15]{0,1:T(8,128)S(1)}, s32[2048,15]{0,1:T(8,128)}, u32[]{:S(2)}) copy-start(s32[2048,15]{0,1:T(8,128)} %param.17) | copy-start | bytes 368644
  76.7 385.4 %all-reduce.6.cloned.1.call-start = ((), (), s32[]{:S(2)}) async-start(), calls=%async_computation.1 | async-start | bytes 5242880 | tf_op jit(solution)/shard_map/psum | solution.py:51
Sparse Core Ops, SparseCore 0:
  76.8 118.6 all-reduce.3
  201.7 260.3 all-reduce.5
where the time goes:
time: 476 us; the launch traced here: 474 us
  waiting for transfers between devices  332 us (70%)
  matrix products  105 us (22%)
  between operations  14.9 us (3%)
  local copies, waits for them, and re-layouts  13.6 us (3%)
  other arithmetic  7.56 us (2%)
    psum x1, waiting for transfers between devices, on_device(): total_one, total_two = lax.psum((grad_one, grad_two), ('clique', 'copy'))  263 us
    dot_general x12, matrix products, one_block(): jnp.dot(counts.astype(jnp.bfloat16), row_grad, preferred_element_type=jnp...  87.3 us
    psum x1, waiting for transfers between devices, on_device(): summed = lax.psum(hot_part, 'clique').astype(jnp.float32)  69.5 us
  transfers between devices with their start and end apart: 2, of which 2 were waited for; matrix products, arithmetic and copies ran while one was open for 10% of the time, Pallas kernels for 0%

commit v1 on v0

v1 whole, which is shorter than its diff:
```python
import functools
import jax
import jax.numpy as jnp
from jax import lax
from jax.experimental import pallas as pl
from jax.experimental.pallas import tpu as pltpu
from jax.sharding import PartitionSpec as P

MESH = pl.DeviceIdType.MESH
BLK = 512
WB = BLK // 8
LANES = 128


def build_counts(idx_ref, block, c_ref):
    k_n, rows = idx_ref.shape
    sub = lax.broadcasted_iota(jnp.int32, (8, LANES), 0)
    for j in range(rows // LANES):
        cols = slice(j * LANES, j * LANES + LANES)
        local = idx_ref[:, cols] - block * BLK
        inside = (local >= 0) & (local < BLK)
        word = jnp.where(inside, local & (WB - 1), -1)
        unit = jnp.left_shift(jnp.ones_like(local), ((local >> 6) & 7) * 4)
        ws = [jnp.broadcast_to(word[k : k + 1], (8, LANES)) for k in range(k_n)]
        us = [jnp.broadcast_to(unit[k : k + 1], (8, LANES)) for k in range(k_n)]
        for pair in range(WB // 16):
            two = []
            for h in range(2):
                at = sub + (pair * 16 + h * 8)
                acc = jnp.where(ws[0] == at, us[0], 0)
                for k in range(1, k_n):
                    acc = acc + jnp.where(ws[k] == at, us[k], 0)
                two.append(acc)
            words = jnp.concatenate(two, 0)
            for b in range(8):
                field = (words >> (4 * b)) & 15
                at = b * WB + pair * 16
                c_ref[at : at + 16, cols] = field.astype(jnp.float32).astype(jnp.bfloat16)


def parts_kernel(
    fanout, cnt_ref, og_hbm, pa_hbm, l2_hbm, hs_hbm, ci_hbm, hp, two_ref, og, pa, l2, hs, ci, rg, c0, c1, sems
):
    rows = og.shape[0]
    tile = 512
    pairs = [(l2_hbm, l2), (og_hbm, og), (pa_hbm, pa), (ci_hbm, ci), (hs_hbm, hs)]
    copies = [pltpu.make_async_copy(s, d, sems.at[i]) for i, (s, d) in enumerate(pairs)]
    for c in copies:
        c.start()
    for c in copies:
        c.wait()
    count = cnt_ref[0]
    two_ref[...] = jnp.zeros_like(two_ref)

    def some_rows(i, carry):
        at = pl.ds(pl.multiple_of(i * tile, tile), tile)
        live = (lax.broadcasted_iota(jnp.int32, (tile, 1), 0) + i * tile) < count
        o = og[at, :]
        masked = jnp.where(live, o, jnp.zeros_like(o))
        p = pa[at, :]
        back = lax.dot_general(
            masked, l2[...], (((1,), (1,)), ((), ())), preferred_element_type=jnp.float32
        )
        rg[at, :] = jnp.where(p > 0, back, 0.0).astype(jnp.bfloat16)
        activ = jnp.maximum(p, jnp.zeros_like(p))
        two_ref[...] += lax.dot_general(
            activ, masked, (((0,), (0,)), ((), ())), preferred_element_type=jnp.float32
        )
        return carry

    lax.fori_loop(0, rows // tile, some_rows, 0)
    n_cold = 4
    n_hot = hp.shape[0] // BLK - n_cold

    def step(idx_ref, block, c_new, c_old, base):
        if idx_ref is not None:
            build_counts(idx_ref, block, c_new)
        p = jnp.dot(c_old[...], rg[...], preferred_element_type=jnp.float32)
        at = pl.ds(pl.multiple_of(base, BLK), BLK)
        hp[at, :] = (p * (1.0 / fanout)).astype(jnp.bfloat16)

    cold = n_hot * BLK
    build_counts(ci, 0, c0)
    step(ci, 1, c1, c0, cold)
    step(ci, 2, c0, c1, cold + BLK)
    step(ci, 3, c1, c0, cold + 2 * BLK)
    step(hs, 0, c0, c1, cold + 3 * BLK)

    def hot(i, carry):
        step(hs, 2 * i + 1, c1, c0, 2 * i * BLK)
        step(hs, 2 * i + 2, c0, c1, (2 * i + 1) * BLK)
        return carry

    lax.fori_loop(0, n_hot // 2 - 1, hot, 0)
    step(hs, n_hot - 1, c1, c0, (n_hot - 2) * BLK)
    step(None, 0, c0, c1, (n_hot - 1) * BLK)


def parts_call(fanout, og, pa, cnt, l2, hs, ci, slots):
    vm = pltpu.VMEM
    rows, dh = og.shape
    return pl.pallas_call(
        functools.partial(parts_kernel, fanout),
        out_shape=(
            jax.ShapeDtypeStruct((slots, dh), jnp.bfloat16),
            jax.ShapeDtypeStruct((dh, dh), jnp.float32),
        ),
        in_specs=[pl.BlockSpec(memory_space=pltpu.SMEM)] + [pl.BlockSpec(memory_space=pl.ANY)] * 5,
        out_specs=[pl.BlockSpec(memory_space=vm)] * 2,
        scratch_shapes=[
            vm((rows, dh), jnp.bfloat16),
            vm((rows, dh), jnp.bfloat16),
            vm((dh, dh), jnp.bfloat16),
            vm((hs.shape[1], rows), jnp.int32),
            vm((ci.shape[1], rows), jnp.int32),
            vm((rows, dh), jnp.bfloat16),
            vm((BLK, rows), jnp.bfloat16),
            vm((BLK, rows), jnp.bfloat16),
            pltpu.SemaphoreType.DMA((5,)),
        ],
        compiler_params=pltpu.CompilerParams(vmem_limit_bytes=48 << 20),
        cost_estimate=pl.CostEstimate(flops=15 * 10**9, bytes_accessed=10**7, transcendentals=0),
    )(cnt, og, pa, l2, hs.T, ci.T)


class Place:
    def __init__(self):
        clique, copy = lax.axis_index("clique"), lax.axis_index("copy")
        self.x, self.y = clique % 4, (clique // 4) * 2 + (copy // 2) % 2
        self.z, self.core = copy // 4, copy % 2
        self.member = self.x * 4 + self.y

    def device(self, x, y, z, core):
        return ((y // 2) * 4 + x, z * 4 + (y % 2) * 2 + core)

    def mate(self):
        return self.device(self.x, self.y, self.z, 1 - self.core)

    def plane(self):
        for dx in range(4):
            for dy in range(4):
                if dx or dy:
                    x, y = (self.x + dx) % 4, (self.y + dy) % 4
                    yield x * 4 + y, self.device(x, y, self.z, self.core)

    def column(self, steps):
        for dz in steps:
            z = (self.z + dz) % 8
            yield z, self.device(self.x, self.y, z, self.core)


def remote(src, dst, send, recv, device):
    return pltpu.make_async_remote_copy(
        src_ref=src, dst_ref=dst, send_sem=send, recv_sem=recv, device_id=device, device_id_type=MESH
    )


def sum_kernel(g_hbm, out_hbm, g, rc, hs, ra, ms, rb, out, sem, c_s, c_r, a_s, a_r, b_s, b_r, d_s, d_r, e_s, e_r, f_s, f_r):
    here = Place()
    half = rc.shape[0]
    per = half // 16
    load = pltpu.make_async_copy(g_hbm, g, sem.at[0])
    load.start()
    barrier = pltpu.get_barrier_semaphore()
    peers = [here.mate()] + [d for _, d in here.plane()] + [d for _, d in here.column(range(1, 8))]
    for d in peers:
        pl.semaphore_signal(barrier, inc=1, device_id=d, device_id_type=MESH)
    pl.semaphore_wait(barrier, len(peers))
    load.wait()
    mine, other = here.core * half, (1 - here.core) * half
    swap = remote(g.at[pl.ds(other, half)], rc, c_s, c_r, here.mate())
    swap.start()
    swap.wait()
    f32 = jnp.float32
    hs[...] = (g[pl.ds(mine, half)].astype(f32) + rc[...].astype(f32)).astype(jnp.bfloat16)
    sent = []
    for q, d in here.plane():
        c = remote(hs.at[pl.ds(q * per, per)], ra.at[here.member], a_s.at[q], a_r.at[here.member], d)
        c.start()
        sent.append(c)
    ra[here.member] = hs[pl.ds(here.member * per, per)]
    for q, d in here.plane():
        remote(hs.at[pl.ds(q * per, per)], ra.at[q], a_s.at[q], a_r.at[q], d).wait_recv()
    ms[...] = jnp.sum(ra[...].astype(f32), axis=0).astype(jnp.bfloat16)
    for z, d in here.column(range(1, 8)):
        at = pl.ds(pl.multiple_of((z % 4) * LANES, LANES), LANES)
        c = remote(ms.at[:, :, at], rb.at[here.z], b_s.at[z], b_r.at[here.z], d)
        c.start()
        sent.append(c)
    part = pl.ds(pl.multiple_of((here.z % 4) * LANES, LANES), LANES)
    rb[here.z] = ms[:, :, part]
    for z, d in here.column(range(1, 8)):
        remote(ms.at[:, :, part], rb.at[z], b_s.at[z], b_r.at[z], d).wait_recv()
    slot = pl.ds(mine + here.member * per, per)
    out[slot, :, part] = jnp.sum(rb[...].astype(f32), axis=0).astype(jnp.bfloat16)
    steps = (1, 7, 6)
    for n, (z, d) in enumerate(here.column(steps)):
        c = remote(out.at[slot, :, part], out.at[slot, :, part], d_s.at[n], d_r.at[n], d)
        c.start()
        sent.append(c)
    for n, (z, d) in enumerate(here.column([8 - s for s in steps])):
        theirs = pl.ds(pl.multiple_of((z % 4) * LANES, LANES), LANES)
        remote(out.at[slot, :, theirs], out.at[slot, :, theirs], d_s.at[n], d_r.at[n], d).wait_recv()
    for q, d in here.plane():
        c = remote(out.at[slot], out.at[slot], e_s.at[q], e_r.at[here.member], d)
        c.start()
        sent.append(c)
    c = remote(out.at[slot], out.at[slot], f_s.at[here.member], f_r.at[here.member], here.mate())
    c.start()
    sent.append(c)
    for q, d in here.plane():
        at = pl.ds(mine + q * per, per)
        remote(out.at[at], out.at[at], e_s.at[q], e_r.at[q], d).wait_recv()
        c = remote(out.at[at], out.at[at], f_s.at[q], f_r.at[q], here.mate())
        c.start()
        sent.append(c)
    for q in range(16):
        at = pl.ds(other + q * per, per)
        remote(out.at[at], out.at[at], f_s.at[q], f_r.at[q], here.mate()).wait_recv()
    for c in sent:
        c.wait_send()
    store = pltpu.make_async_copy(out, out_hbm, sem.at[1])
    store.start()
    store.wait()


def sum_call(g):
    vm, dma = pltpu.VMEM, pltpu.SemaphoreType.DMA
    units, _, dh = g.shape
    half, per, bf16 = units // 2, units // 32, jnp.bfloat16
    return pl.pallas_call(
        sum_kernel,
        out_shape=jax.ShapeDtypeStruct(g.shape, bf16),
        in_specs=[pl.BlockSpec(memory_space=pl.ANY)],
        out_specs=pl.BlockSpec(memory_space=pl.ANY),
        scratch_shapes=[
            vm(g.shape, bf16),
            vm((half, 8, dh), bf16),
            vm((half, 8, dh), bf16),
            vm((16, per, 8, dh), bf16),
            vm((per, 8, dh), bf16),
            vm((8, per, 8, LANES), bf16),
            vm(g.shape, bf16),
            dma((2,)),
            dma,
            dma,
            dma((16,)),
            dma((16,)),
            dma((8,)),
            dma((8,)),
            dma((3,)),
            dma((3,)),
            dma((16,)),
            dma((16,)),
            dma((16,)),
            dma((16,)),
        ],
        compiler_params=pltpu.CompilerParams(
            collective_id=0, has_side_effects=True, vmem_limit_bytes=32 << 20
        ),
    )(g)


def on_device(
    out_grad, pre_act, batch_count, layer_two, hot_slots, cold_index, hot_feats, cold_feats
):
    fanout = hot_slots.shape[1] + cold_index.shape[1]
    din, dh = hot_feats.shape[1], out_grad.shape[1]
    hot_all = lax.all_gather(hot_feats, "clique", axis=0, tiled=True)
    hot = hot_all.shape[0]
    slots = hot + cold_feats.shape[0]
    parts, grad_two = parts_call(
        fanout, out_grad, pre_act, batch_count, layer_two, hot_slots, cold_index, slots
    )
    grad_one = jnp.dot(hot_all.T, parts[:hot], preferred_element_type=jnp.float32)
    grad_one = grad_one + jnp.dot(
        cold_feats.T, parts[hot:], preferred_element_type=jnp.float32
    )
    both = jnp.concatenate([grad_one, grad_two], 0).astype(jnp.bfloat16)
    total = sum_call(both.reshape(-1, 8, dh)).reshape(-1, dh).astype(jnp.float32)
    return total[:din], total[din:]


def solution(mesh):
    placed = (
        P(("clique", "copy"), None),
        P(("clique", "copy"), None),
        P(("clique", "copy")),
        P(),
        P(("clique", "copy"), None),
        P(("clique", "copy"), None),
        P("clique", None),
        P(("clique", "copy"), None),
    )
    return jax.shard_map(
        on_device, mesh=mesh, in_specs=placed, out_specs=(P(), P()), check_vma=False
    )
```

time: 476 us -> 173 us (0.36)
  waiting for transfers between devices: 332 us -> 60.7 us
  matrix products: 105 us -> 10.6 us
  Pallas kernels: 0 us -> 70.1 us
  other arithmetic: 7.56 us -> 2.35 us
    psum x2 -> x0, waiting for transfers between devices: 332 us -> none  [the longest x1 263 us: on_device(): total_one, total_two = lax.psum((grad_one, grad_two), ('clique', 'copy'))]
    dot_general x16 -> x2, matrix products: 105 us -> 10.6 us  [the longest x1 7.09 us: on_device(): jnp.dot(hot_all.T, parts[:hot], preferred_element_type=jnp.float32)]
    pallas_call x0 -> x2, Pallas kernels: none -> 70.1 us  [the longest x1 39 us: sum_call(): pl.pallas_call(sum_kernel, out_shape=jax.ShapeDtypeStruct(g.shape, bf16),...]
    all_gather x0 -> x1, waiting for transfers between devices: none -> 60 us  [on_device(): hot_all = lax.all_gather(hot_feats, 'clique', axis=0, tiled=True)]
    dynamic_slice x12 -> x0, local copies, waits for them, and re-layouts: 7.56 us -> none  [table_sums(): parts = lax.map(one_block, starts)]
    add x12 -> x0, other arithmetic: 7.54 us -> none  [one_block(): wanted = start + offsets]
  transfers between devices with their start and end apart: 2 -> 1, of which waited for: 2 -> 1; matrix products, arithmetic and copies ran while one was open for 10% -> 2% of each run, Pallas kernels for 0% -> 18%
where the time goes in v1:
time: 173 us
  Pallas kernels  70.1 us (41%)
  waiting for transfers between devices  60.7 us (35%)
  between operations  15 us (9%)
  local copies, waits for them, and re-layouts  14.1 us (8%)
  matrix products  10.6 us (6%)
  other arithmetic  2.35 us (1%)
    all_gather x1, waiting for transfers between devices, on_device(): hot_all = lax.all_gather(hot_feats, 'clique', axis=0, tiled=True)  60 us
    pallas_call x1, Pallas kernels, sum_call(): pl.pallas_call(sum_kernel, out_shape=jax.ShapeDtypeStruct(g.shape, bf16),...  39 us
    pallas_call x1, Pallas kernels, parts_call(): pl.pallas_call(functools.partial(parts_kernel, fanout), out_shape=(jax.Sh...  31.1 us
    unnamed x16, local copies, waits for them, and re-layouts  7.35 us
    dot_general x1, matrix products, on_device(): jnp.dot(hot_all.T, parts[:hot], preferred_element_type=jnp.float32)  7.09 us
    dot_general x1, matrix products, on_device(): jnp.dot(cold_feats.T, parts[hot:], preferred_element_type=jnp.float32)  3.49 us
  transfers between devices with their start and end apart: 1, of which 1 were waited for; matrix products, arithmetic and copies ran while one was open for 2% of the time, Pallas kernels for 18%

profile of v1, /device:TPU:1, one launch (start us, length us, event | category | flops | bytes accessed | tf_op | source)
XLA Modules:
  0.0 172.8 jit_solution(186250474727745592)
XLA Ops:
  7.2 0.0 copy-start
  7.2 0.0 all-gather.2.cloned.1.call-start
  7.2 0.7 all-gather.2.cloned.1.call-update
  8.8 0.0 copy-start.2
  8.8 1.6 copy-done.2
  10.4 0.0 copy-start.3
  10.4 1.6 copy-done.3
  12.0 0.0 copy-start.4
  12.0 1.0 copy-done.4
  13.0 0.0 copy-start.5
  13.0 0.9 copy-done.5
  13.9 0.0 copy-start.6
  13.9 0.9 copy-done.6
  14.8 31.1 %shard_map.95 = (bf16[6144,512]{1,0:T(8,128)(2,1)}, f32[512,512]{1,0:T(8,128)S(1)}) custom-call(s32[1]{0:T(128)S(6)} %copy.12.cnt_ref, bf16[2048,512]{1,0:T(8,128)(2,1)S(1)} %copy-done.2, bf16[2048,512]{1,0:T(8,128)(2,1)S(1)} %copy-done.3, bf16[512,512]{1,0:T(8,128)(2,1)S(1)} %copy-done.4, s32[10,2048]{1,0:T(8,128)S(1)} %bitcast.12, s32[15,2048]{1,0:T(8,128)S(1)} %bitcast.13), custom_call_target="tpu_custom_call" | custom-call | flops 15000000512 | bytes 10000000 | tf_op jit(solution)/shard_map/pallas_call | solution.py:102
  45.9 0.9 convert.8
  46.8 2.0 %copy.10 = bf16[512,512]{0,1:T(8,128)(2,1)} copy(bf16[512,512]{1,0:T(8,128)(2,1)} %convert.8) | data formatting | bytes 1048576 | tf_op jit(solution)/shard_map/convert.1
  48.8 60.0 %all-gather.2.cloned.1.call-done = bf16[4096,768]{1,0:T(8,128)(2,1)} async-done(((bf16[512,768]{1,0:T(8,128)(2,1)}), bf16[4096,768]{1,0:T(8,128)(2,1)}) %all-gather.2.cloned.1.call-update) | async-done | bytes 6291472 | tf_op jit(solution)/shard_map/all_gather | solution.py:269
  108.8 7.1 %fusion = f32[512,768]{1,0:T(8,128)S(1)} fusion(bf16[4096,768]{1,0:T(8,128)(2,1)} %all-gather.2.cloned.1.call-done, bf16[6144,512]{1,0:T(8,128)(2,1)} %get-tuple-element.4), kind=kOutput, calls=%fused_computation | convolution fusion | flops 3221225472 | bytes 12058624 | tf_op jit(solution)/shard_map/dot_general | solution.py:275
  115.9 0.0 copy-done
  115.9 0.0 copy-start.7
  115.9 3.5 %fusion.6 = bf16[768,512]{0,1:T(8,128)(2,1)S(1)} fusion(f32[512,768]{1,0:T(8,128)S(1)} %fusion, bf16[2048,768]{1,0:T(8,128)(2,1)S(1)} %copy-done, bf16[6144,512]{1,0:T(8,128)(2,1)} %get-tuple-element.4), kind=kOutput, calls=%fused_computation.7 | convolution fusion | flops 1611399168 | bytes 7602176 | tf_op jit(solution)/shard_map/dot_general | solution.py:276
  119.4 0.0 copy-done.7
  119.4 1.1 pad_maximum_fusion
  120.6 2.4 %copy.11 = bf16[1280,512]{1,0:T(8,128)(2,1)} copy(bf16[1280,512]{0,1:T(8,128)(2,1)} %pad_maximum_fusion) | data formatting | bytes 2621440 | tf_op jit(solution)/shard_map/concatenate | solution.py:279
  123.0 0.0 copy-start.1
  123.0 1.3 copy-done.1
  124.3 39.0 %shard_map.96 = bf16[160,8,512]{2,1,0:T(8,128)(2,1)S(1)} custom-call(bf16[160,8,512]{2,1,0:T(8,128)(2,1)S(1)} %bitcast.11), custom_call_target="tpu_custom_call" | custom-call | tf_op jit(solution)/shard_map/pallas_call | solution.py:231
  163.3 0.3 convert_element_type.10
  163.7 1.3 slice_bitcast_fusion
  164.9 1.0 slice_bitcast_fusion.1
Async XLA Ops:
  7.2 108.7 %copy-start = (bf16[2048,768]{1,0:T(8,128)(2,1)S(1)}, bf16[2048,768]{1,0:T(8,128)(2,1)}, u32[]{:S(2)}) copy-start(bf16[2048,768]{1,0:T(8,128)(2,1)} %param.15) | copy-start | bytes 9437188
  7.2 101.6 %all-gather.2.cloned.1.call-start = ((), (), s32[]{:S(2)}) async-start(), calls=%async_computation | async-start | bytes 7077888 | tf_op jit(solution)/shard_map/all_gather | solution.py:269
  8.8 1.6 copy-start.2
  10.4 1.6 copy-start.3
  12.0 1.0 copy-start.4
  13.0 0.9 copy-start.5
  13.9 0.9 copy-start.6
  115.9 3.5 %copy-start.7 = (bf16[512,512]{0,1:T(8,128)(2,1)S(1)}, bf16[512,512]{0,1:T(8,128)(2,1)}, u32[]{:S(2)}) copy-start(bf16[512,512]{0,1:T(8,128)(2,1)} %copy.10) | copy-start | bytes 1572868
  123.0 1.3 copy-start.1
Sparse Core Ops, SparseCore 0:
  10.6 98.1 all-gather.1

commit v2 on v0

v2 whole, which is shorter than its diff:
```python
import functools
import jax
import jax.numpy as jnp
from jax import lax
from jax.experimental import pallas as pl
from jax.experimental.pallas import tpu as pltpu
from jax.sharding import PartitionSpec as P

MESH = pl.DeviceIdType.MESH
BLK = 512
WB = BLK // 8
LANES = 128


def build_counts(idx_ref, block, c_ref):
    k_n, rows = idx_ref.shape
    sub = lax.broadcasted_iota(jnp.int32, (8, LANES), 0)
    for j in range(rows // LANES):
        cols = slice(j * LANES, j * LANES + LANES)
        local = idx_ref[:, cols] - block * BLK
        inside = (local >= 0) & (local < BLK)
        word = jnp.where(inside, local & (WB - 1), -1)
        unit = jnp.left_shift(jnp.ones_like(local), ((local >> 6) & 7) * 4)
        ws = [jnp.broadcast_to(word[k : k + 1], (8, LANES)) for k in range(k_n)]
        us = [jnp.broadcast_to(unit[k : k + 1], (8, LANES)) for k in range(k_n)]
        for pair in range(WB // 16):
            two = []
            for h in range(2):
                at = sub + (pair * 16 + h * 8)
                acc = jnp.where(ws[0] == at, us[0], 0)
                for k in range(1, k_n):
                    acc = acc + jnp.where(ws[k] == at, us[k], 0)
                two.append(acc)
            words = jnp.concatenate(two, 0)
            for b in range(8):
                field = (words >> (4 * b)) & 15
                at = b * WB + pair * 16
                c_ref[at : at + 16, cols] = field.astype(jnp.float32).astype(jnp.bfloat16)


class Place:
    def __init__(self):
        clique, copy = lax.axis_index("clique"), lax.axis_index("copy")
        self.x, self.y = clique % 4, (clique // 4) * 2 + (copy // 2) % 2
        self.z, self.core = copy // 4, copy % 2
        self.member = self.x * 4 + self.y

    def device(self, x, y, z, core):
        return ((y // 2) * 4 + x, z * 4 + (y % 2) * 2 + core)

    def mate(self):
        return self.device(self.x, self.y, self.z, 1 - self.core)

    def plane(self):
        for dx in range(4):
            for dy in range(4):
                if dx or dy:
                    x, y = (self.x + dx) % 4, (self.y + dy) % 4
                    yield x * 4 + y, self.device(x, y, self.z, self.core)

    def column(self, steps):
        for dz in steps:
            z = (self.z + dz) % 8
            yield z, self.device(self.x, self.y, z, self.core)


def remote(src, dst, send, recv, device):
    return pltpu.make_async_remote_copy(
        src_ref=src, dst_ref=dst, send_sem=send, recv_sem=recv, device_id=device, device_id_type=MESH
    )


class Gather:
    def __init__(self, here, own, feats, send, recv):
        h, n = BLK // 2, iter(range(15))
        self.out, self.into, self.own = [], [], own
        right = here.device((here.x + 1) % 4, here.y, here.z, here.core)
        left = here.device((here.x + 3) % 4, here.y, here.z, here.core)
        across = here.device(here.x, 3 - here.y, here.z, here.core)
        hi = here.y // 2

        def rows(dx, flip, core, start=0, count=h):
            block = (1 - hi if flip else hi) * 4 + (here.x + dx) % 4
            return feats.at[pl.ds(pl.multiple_of(block * BLK + core * h + start, h // 2), count), :]

        def add(to, dx, flip, got_dx, got_flip, start=0, count=h, first=False):
            i = next(n)
            dst = rows(dx, flip, here.core, start, count)
            src = own.at[pl.ds(pl.multiple_of(here.core * h, h), h), :] if first else dst
            self.out.append(remote(src, dst, send.at[i], recv.at[i], to))
            core = here.core if to is not mate else 1 - here.core
            got = rows(got_dx, got_flip, core, start, count)
            self.into.append(remote(got, got, send.at[i], recv.at[i], to))

        mate = here.mate()
        q = h // 2
        add(right, 0, False, 3, False, first=True)
        add(left, 0, False, 1, False, first=True)
        add(across, 0, False, 0, True, first=True)
        add(right, 3, False, 2, False, 0, q)
        add(mate, 3, False, 3, False)
        add(left, 1, False, 2, False, q, q)
        add(mate, 1, False, 1, False)
        add(right, 0, True, 3, True)
        add(left, 0, True, 1, True)
        add(mate, 0, True, 0, True)
        add(across, 2, False, 2, True)
        add(mate, 2, False, 2, False)
        add(mate, 3, True, 3, True)
        add(mate, 1, True, 1, True)
        add(mate, 2, True, 2, True)

    def run(self, steps):
        for got, go in steps:
            for i in got:
                self.into[i].wait_recv()
            for i in go:
                self.out[i].start()

    def first(self):
        self.run([((), (0, 1, 2))])

    def second(self):
        self.run([((0,), (3,)), ((1,), (5,)), ((2,), (7, 8)), ((), (4, 6, 9))])

    def third(self):
        self.run([((3, 5), (10, 11)), ((7,), (12,)), ((8,), (13,))])

    def fourth(self):
        self.run([((10,), (14,)), ((4, 6, 9, 11, 12, 13, 14), ())])

    def finish(self):
        for c in self.out:
            c.wait_send()


class Sum:
    def __init__(self, here, bufs, sems):
        self.here = here
        self.g, self.rc, self.hs, self.ra, self.ms, self.rb, self.out = bufs
        c_s, c_r, a_s, a_r, b_s, b_r, d_s, d_r, e_s, e_r, f_s, f_r = sems
        g, rc, hs, ra, ms, rb, out = bufs
        half = rc.shape[0]
        per = half // 16
        mate, me = here.mate(), here.member
        plane = list(here.plane())
        column = list(here.column(range(1, 8)))
        self.mine, self.other = here.core * half, (1 - here.core) * half
        self.half, self.per = half, per
        self.swap = remote(g.at[pl.ds(self.other, half)], rc, c_s, c_r, mate)
        self.to_plane = [
            remote(hs.at[pl.ds(q * per, per)], ra.at[me], a_s.at[q], a_r.at[me], d) for q, d in plane
        ]
        self.of_plane = [
            remote(hs.at[pl.ds(q * per, per)], ra.at[q], a_s.at[q], a_r.at[q], d) for q, d in plane
        ]

        def block(z):
            return pl.ds(pl.multiple_of((z % 4) * LANES, LANES), LANES)

        self.part = part = block(here.z)
        self.to_column = [
            remote(ms.at[:, :, block(z)], rb.at[here.z], b_s.at[z], b_r.at[here.z], d) for z, d in column
        ]
        self.of_column = [
            remote(ms.at[:, :, part], rb.at[z], b_s.at[z], b_r.at[z], d) for z, d in column
        ]
        self.slot = slot = pl.ds(self.mine + me * per, per)
        steps = (1, 7, 6)
        mine = out.at[slot, :, part]
        self.back_to = [
            remote(mine, mine, d_s.at[n], d_r.at[n], d) for n, (z, d) in enumerate(here.column(steps))
        ]
        self.back_of = []
        for n, (z, d) in enumerate(here.column([8 - s for s in steps])):
            theirs = out.at[slot, :, block(z)]
            self.back_of.append(remote(theirs, theirs, d_s.at[n], d_r.at[n], d))
        self.home_to, self.home_of, self.pass_to, self.pass_of = [], [], [], []
        for q, d in plane:
            at = out.at[pl.ds(self.mine + q * per, per)]
            self.home_to.append(remote(out.at[slot], out.at[slot], e_s.at[q], e_r.at[me], d))
            self.home_of.append(remote(at, at, e_s.at[q], e_r.at[q], d))
            self.pass_to.append(remote(at, at, f_s.at[q], f_r.at[q], mate))
        self.own_to = remote(out.at[slot], out.at[slot], f_s.at[me], f_r.at[me], mate)
        for q in range(16):
            at = out.at[pl.ds(self.other + q * per, per)]
            self.pass_of.append(remote(at, at, f_s.at[q], f_r.at[q], mate))

    def to_pair(self):
        self.swap.start()

    def to_the_plane(self):
        f32 = jnp.float32
        self.swap.wait_recv()
        both = self.g[pl.ds(self.mine, self.half)].astype(f32) + self.rc[...].astype(f32)
        self.hs[...] = both.astype(jnp.bfloat16)
        for c in self.to_plane:
            c.start()
        self.ra[self.here.member] = self.hs[pl.ds(self.here.member * self.per, self.per)]

    def to_the_column(self):
        for c in self.of_plane:
            c.wait_recv()
        self.ms[...] = jnp.sum(self.ra[...].astype(jnp.float32), axis=0).astype(jnp.bfloat16)
        for c in self.to_column:
            c.start()
        self.rb[self.here.z] = self.ms[:, :, self.part]

    def back_in_column(self):
        for c in self.of_column:
            c.wait_recv()
        total = jnp.sum(self.rb[...].astype(jnp.float32), axis=0).astype(jnp.bfloat16)
        self.out[self.slot, :, self.part] = total
        for c in self.back_to:
            c.start()

    def back_in_plane(self):
        for c in self.back_of:
            c.wait_recv()
        for c in self.home_to:
            c.start()
        self.own_to.start()

    def back_to_pair(self):
        for c, then in zip(self.home_of, self.pass_to):
            c.wait_recv()
            then.start()

    def received(self):
        for c in self.pass_of:
            c.wait_recv()

    def finish(self):
        sent = [self.swap, *self.to_plane, *self.to_column, *self.back_to, *self.home_to, *self.pass_to]
        for c in [*sent, self.own_to]:
            c.wait_send()


def whole_kernel(
    fanout, cnt_ref, og_hbm, pa_hbm, l2_hbm, hs_hbm, ci_hbm, hf_hbm, cf_hbm, one_hbm, two_hbm,
    og, pa, l2, hs, ci, feats, rg, hp, c0, c1, two, sems, g_send, g_recv, one_bufs, one_sems, two_bufs, two_sems,
):
    rows, dh = og.shape
    din = feats.shape[1]
    tile = 512
    hot_n = hf_hbm.shape[0] * 8
    here = Place()
    gather = Gather(here, hf_hbm, feats, g_send, g_recv)
    sum_one = Sum(here, one_bufs, one_sems)
    sum_two = Sum(here, two_bufs, two_sems)
    home = pl.ds(pl.multiple_of(lax.axis_index("clique") * BLK, BLK), BLK)
    pairs = [
        (l2_hbm, l2),
        (og_hbm, og),
        (pa_hbm, pa),
        (ci_hbm, ci),
        (hs_hbm, hs),
        (cf_hbm, feats.at[pl.ds(hot_n, cf_hbm.shape[0]), :]),
        (hf_hbm, feats.at[home, :]),
    ]
    copies = [pltpu.make_async_copy(s, d, sems.at[i]) for i, (s, d) in enumerate(pairs)]
    barrier = pltpu.get_barrier_semaphore()
    peers = [here.mate()] + [d for _, d in here.plane()] + [d for _, d in here.column(range(1, 8))]
    for d in peers:
        pl.semaphore_signal(barrier, inc=1, device_id=d, device_id_type=MESH)
    for c in copies:
        c.start()
    pl.semaphore_wait(barrier, len(peers))
    gather.first()
    for c in copies[:3]:
        c.wait()
    count = cnt_ref[0]
    two[...] = jnp.zeros_like(two)

    def some_rows(i, carry):
        at = pl.ds(pl.multiple_of(i * tile, tile), tile)
        live = (lax.broadcasted_iota(jnp.int32, (tile, 1), 0) + i * tile) < count
        o = og[at, :]
        masked = jnp.where(live, o, jnp.zeros_like(o))
        p = pa[at, :]
        back = lax.dot_general(
            masked, l2[...], (((1,), (1,)), ((), ())), preferred_element_type=jnp.float32
        )
        rg[at, :] = jnp.where(p > 0, back, 0.0).astype(jnp.bfloat16)
        activ = jnp.maximum(p, jnp.zeros_like(p))
        two[...] += lax.dot_general(
            activ, masked, (((0,), (0,)), ((), ())), preferred_element_type=jnp.float32
        )
        return carry

    lax.fori_loop(0, rows // tile, some_rows, 0)
    sum_two.g[...] = two[...].reshape(dh // 8, 8, dh).astype(jnp.bfloat16)
    sum_two.to_pair()
    for c in copies[3:5]:
        c.wait()
    n_hot = hot_n // BLK

    def step(idx_ref, block, c_new, c_old, base):
        if idx_ref is not None:
            build_counts(idx_ref, block, c_new)
        p = jnp.dot(c_old[...], rg[...], preferred_element_type=jnp.float32)
        at = pl.ds(pl.multiple_of(base, BLK), BLK)
        hp[at, :] = (p * (1.0 / fanout)).astype(jnp.bfloat16)

    build_counts(ci, 0, c0)
    step(ci, 1, c1, c0, hot_n)
    sum_two.to_the_plane()
    step(ci, 2, c0, c1, hot_n + BLK)
    gather.second()
    step(ci, 3, c1, c0, hot_n + 2 * BLK)
    step(hs, 0, c0, c1, hot_n + 3 * BLK)
    sum_two.to_the_column()

    def hot(i, carry):
        step(hs, 2 * i + 1, c1, c0, 2 * i * BLK)
        step(hs, 2 * i + 2, c0, c1, (2 * i + 1) * BLK)

        @pl.when(i == 0)
        def _():
            sum_two.back_in_column()

        @pl.when(i == 1)
        def _():
            gather.third()
            sum_two.back_in_plane()

        @pl.when(i == 2)
        def _():
            sum_two.back_to_pair()

        return carry

    lax.fori_loop(0, n_hot // 2 - 1, hot, 0)
    step(hs, n_hot - 1, c1, c0, (n_hot - 2) * BLK)
    step(None, 0, c0, c1, (n_hot - 1) * BLK)
    sum_two.received()
    two_out = pltpu.make_async_copy(sum_two.out, two_hbm, sems.at[7])
    two_out.start()
    for c in copies[5:]:
        c.wait()
    gather.fourth()

    def some_sums(core):
        at = pl.ds(pl.multiple_of(core * (din // 2), LANES), din // 2)
        sums = lax.dot_general(
            feats[:, at], hp[...], (((0,), (0,)), ((), ())), preferred_element_type=jnp.float32
        )
        half = sum_one.half
        sum_one.g[pl.ds(core * half, half)] = sums.reshape(half, 8, dh).astype(jnp.bfloat16)

    some_sums(1 - here.core)
    sum_one.to_pair()
    some_sums(here.core)
    sum_one.to_the_plane()
    sum_one.to_the_column()
    sum_one.back_in_column()
    sum_one.back_in_plane()
    sum_one.back_to_pair()
    sum_one.received()
    one_out = pltpu.make_async_copy(sum_one.out, one_hbm, sems.at[8])
    one_out.start()
    gather.finish()
    sum_two.finish()
    sum_one.finish()
    two_out.wait()
    one_out.wait()


def sum_scratch(rows, dh):
    vm, dma, bf16 = pltpu.VMEM, pltpu.SemaphoreType.DMA, jnp.bfloat16
    units = rows // 8
    half, per = units // 2, units // 32
    bufs = (
        vm((units, 8, dh), bf16),
        vm((half, 8, dh), bf16),
        vm((half, 8, dh), bf16),
        vm((16, per, 8, dh), bf16),
        vm((per, 8, dh), bf16),
        vm((8, per, 8, LANES), bf16),
        vm((units, 8, dh), bf16),
    )
    sems = [dma, dma] + [dma((n,)) for n in (16, 16, 8, 8, 3, 3, 16, 16, 16, 16)]
    return bufs, tuple(sems)


def whole_call(fanout, og, pa, cnt, l2, hs, ci, hf, cf):
    vm, dma = pltpu.VMEM, pltpu.SemaphoreType.DMA
    hbm = pl.BlockSpec(memory_space=pltpu.HBM)
    bf16 = jnp.bfloat16
    rows, dh = og.shape
    din = hf.shape[1]
    slots = hf.shape[0] * 8 + cf.shape[0]
    one_bufs, one_sems = sum_scratch(din, dh)
    two_bufs, two_sems = sum_scratch(dh, dh)
    return pl.pallas_call(
        functools.partial(whole_kernel, fanout),
        out_shape=(
            jax.ShapeDtypeStruct((din // 8, 8, dh), bf16),
            jax.ShapeDtypeStruct((dh // 8, 8, dh), bf16),
        ),
        in_specs=[pl.BlockSpec(memory_space=pltpu.SMEM)] + [hbm] * 7,
        out_specs=[hbm] * 2,
        scratch_shapes=[
            vm((rows, dh), bf16),
            vm((rows, dh), bf16),
            vm((dh, dh), bf16),
            vm((hs.shape[1], rows), jnp.int32),
            vm((ci.shape[1], rows), jnp.int32),
            vm((slots, din), bf16),
            vm((rows, dh), bf16),
            vm((slots, dh), bf16),
            vm((BLK, rows), bf16),
            vm((BLK, rows), bf16),
            vm((dh, dh), jnp.float32),
            dma((9,)),
            dma((15,)),
            dma((15,)),
            one_bufs,
            one_sems,
            two_bufs,
            two_sems,
        ],
        compiler_params=pltpu.CompilerParams(
            collective_id=0, has_side_effects=True, vmem_limit_bytes=56 << 20
        ),
    )(cnt, og, pa, l2, hs.T, ci.T, hf, cf)


def on_device(
    out_grad, pre_act, batch_count, layer_two, hot_slots, cold_index, hot_feats, cold_feats
):
    fanout = hot_slots.shape[1] + cold_index.shape[1]
    one, two = whole_call(
        fanout, out_grad, pre_act, batch_count, layer_two, hot_slots, cold_index, hot_feats, cold_feats
    )
    dh = out_grad.shape[1]
    return one.reshape(-1, dh).astype(jnp.float32), two.reshape(-1, dh).astype(jnp.float32)


def solution(mesh):
    placed = (
        P(("clique", "copy"), None),
        P(("clique", "copy"), None),
        P(("clique", "copy")),
        P(),
        P(("clique", "copy"), None),
        P(("clique", "copy"), None),
        P("clique", None),
        P(("clique", "copy"), None),
    )
    return jax.shard_map(
        on_device, mesh=mesh, in_specs=placed, out_specs=(P(), P()), check_vma=False
    )
```

time: 476 us -> 87.7 us (0.18)
  waiting for transfers between devices: 332 us -> 0 us
  matrix products: 105 us -> 0 us
  Pallas kernels: 0 us -> 82.6 us
  between operations: 14.9 us -> 1.3 us
  local copies, waits for them, and re-layouts: 13.6 us -> 0.01 us
    psum x2 -> x0, waiting for transfers between devices: 332 us -> none  [the longest x1 263 us: on_device(): total_one, total_two = lax.psum((grad_one, grad_two), ('clique', 'copy'))]
    dot_general x16 -> x0, matrix products: 105 us -> none  [the longest x12 87.3 us: one_block(): jnp.dot(counts.astype(jnp.bfloat16), row_grad, preferred_element_type=jnp...]
    pallas_call x0 -> x1, Pallas kernels: none -> 82.6 us  [whole_call(): pl.pallas_call(functools.partial(whole_kernel, fanout), out_shape=(jax.Sh...]
    dynamic_slice x12 -> x0, local copies, waits for them, and re-layouts: 7.56 us -> none  [table_sums(): parts = lax.map(one_block, starts)]
    add x12 -> x0, other arithmetic: 7.54 us -> none  [one_block(): wanted = start + offsets]
    unnamed x8 -> x2, local copies, waits for them, and re-layouts: 5.3 us -> 0.01 us
  transfers between devices with their start and end apart: 2 -> 0, of which waited for: 2 -> 0; matrix products, arithmetic and copies ran while one was open for 10% -> 0% of each run, Pallas kernels for 0% -> 0%
where the time goes in v2:
time: 87.7 us; the launch traced here: 87.6 us
  Pallas kernels  82.6 us (94%)
  other arithmetic  3.65 us (4%)
  between operations  1.3 us (1%)
    pallas_call x1, Pallas kernels, whole_call(): pl.pallas_call(functools.partial(whole_kernel, fanout), out_shape=(jax.Sh...  82.6 us
    convert_element_type x1, other arithmetic, on_device(): one.reshape(-1, dh).astype(jnp.float32)  2.55 us

profile of v2, /device:TPU:1, one launch (start us, length us, event | category | flops | bytes accessed | tf_op | source)
XLA Modules:
  0.0 87.6 jit_solution(18144650653904037261)
XLA Ops:
  1.3 82.6 %shard_map.95 = (bf16[96,8,512]{2,1,0:T(8,128)(2,1)}, bf16[64,8,512]{2,1,0:T(8,128)(2,1)}) custom-call(s32[1]{0:T(128)S(6)} %copy.10.cnt_ref, bf16[2048,512]{1,0:T(8,128)(2,1)} %og_hbm.1, bf16[2048,512]{1,0:T(8,128)(2,1)} %pa_hbm.1, bf16[512,512]{1,0:T(8,128)(2,1)} %l2_hbm.1, s32[10,2048]{1,0:T(8,128)} %bitcast.8, s32[15,2048]{1,0:T(8,128)} %bitcast.9, ...), custom_call_target="tpu_custom_call" | custom-call | tf_op jit(solution)/shard_map/pallas_call | solution.py:395
  83.9 0.0 copy-start
  83.9 2.5 %bitcast_convert_fusion = f32[768,512]{1,0:T(8,128)} fusion(bf16[96,8,512]{2,1,0:T(8,128)(2,1)} %get-tuple-element.4), kind=kLoop, calls=%fused_computation | loop fusion | flops 393216 | bytes 2359296 | tf_op jit(solution)/shard_map/convert_element_type | solution.py:437
  86.5 0.0 copy-done
  86.5 1.1 %bitcast_convert_fusion.1 = f32[512,512]{1,0:T(8,128)} fusion(bf16[64,8,512]{2,1,0:T(8,128)(2,1)S(1)} %copy-done), kind=kLoop, calls=%fused_computation.1 | loop fusion | flops 262144 | bytes 1572864 | tf_op jit(solution)/shard_map/convert_element_type | solution.py:437
Async XLA Ops:
  83.9 2.6 %copy-start = (bf16[64,8,512]{2,1,0:T(8,128)(2,1)S(1)}, bf16[64,8,512]{2,1,0:T(8,128)(2,1)}, u32[]{:S(2)}) copy-start(bf16[64,8,512]{2,1,0:T(8,128)(2,1)} %get-tuple-element.5) | copy-start | bytes 1572868

commit v3 on v2

--- a/solution.py
+++ b/solution.py
@@ -8,34 +8,53 @@
 
 MESH = pl.DeviceIdType.MESH
 BLK = 512
-WB = BLK // 8
+FIELDS = 16
+WB = BLK // FIELDS
 LANES = 128
 
 
-def build_counts(idx_ref, block, c_ref):
-    k_n, rows = idx_ref.shape
-    sub = lax.broadcasted_iota(jnp.int32, (8, LANES), 0)
+def split_indices(idx_ref, unit_ref):
+    idx = idx_ref[...]
+    unit_ref[...] = jnp.left_shift(jnp.ones_like(idx), ((idx >> 5) & 15) * 2)
+    idx_ref[...] = (idx >> 9) * WB + (idx & (WB - 1))
+
+
+def build_counts(word_ref, unit_ref, block, c_ref):
+    k_n, rows = word_ref.shape
+    assert k_n <= 15
+    sub = lax.broadcasted_iota(jnp.int32, (8, LANES), 0) + block * WB
+    low = jnp.full((8, LANES), 0x33333333, jnp.int32)
     for j in range(rows // LANES):
         cols = slice(j * LANES, j * LANES + LANES)
-        local = idx_ref[:, cols] - block * BLK
-        inside = (local >= 0) & (local < BLK)
-        word = jnp.where(inside, local & (WB - 1), -1)
-        unit = jnp.left_shift(jnp.ones_like(local), ((local >> 6) & 7) * 4)
-        ws = [jnp.broadcast_to(word[k : k + 1], (8, LANES)) for k in range(k_n)]
-        us = [jnp.broadcast_to(unit[k : k + 1], (8, LANES)) for k in range(k_n)]
-        for pair in range(WB // 16):
-            two = []
-            for h in range(2):
-                at = sub + (pair * 16 + h * 8)
-                acc = jnp.where(ws[0] == at, us[0], 0)
-                for k in range(1, k_n):
-                    acc = acc + jnp.where(ws[k] == at, us[k], 0)
-                two.append(acc)
-            words = jnp.concatenate(two, 0)
-            for b in range(8):
-                field = (words >> (4 * b)) & 15
-                at = b * WB + pair * 16
-                c_ref[at : at + 16, cols] = field.astype(jnp.float32).astype(jnp.bfloat16)
+        ws = [jnp.broadcast_to(word_ref[k : k + 1, cols], (8, LANES)) for k in range(k_n)]
+        us = [jnp.broadcast_to(unit_ref[k : k + 1, cols], (8, LANES)) for k in range(k_n)]
+        halves = ([], [])
+        for t in range(WB // 8):
+            at = sub + t * 8
+            even, odd = [], []
+            for first in range(0, k_n, 3):
+                acc = None
+                for k in range(first, min(first + 3, k_n)):
+                    hit = jnp.where(ws[k] == at, us[k], 0)
+                    acc = hit if acc is None else acc + hit
+                even.append(acc & low)
+                odd.append((acc >> 2) & low)
+            halves[0].append(functools.reduce(lambda p, q: p + q, even))
+            halves[1].append(functools.reduce(lambda p, q: p + q, odd))
+        for parity in range(2):
+            for t in range(0, WB // 8, 2):
+                words = jnp.concatenate(halves[parity][t : t + 2], 0)
+                for b in range(8):
+                    if b < 7:
+                        field = words & (15 << (4 * b))
+                    else:
+                        field = lax.shift_right_logical(words, jnp.full_like(words, 28))
+                    at = (2 * b + parity) * WB + t * 8
+                    c_ref[at : at + 16, cols] = field.astype(jnp.float32).astype(jnp.bfloat16)
+
+
+def field_scale(b):
+    return 2.0 ** (-4 * b) if b < 7 else 1.0
 
 
 class Place:
@@ -72,45 +91,59 @@
 
 class Gather:
     def __init__(self, here, own, feats, send, recv):
-        h, n = BLK // 2, iter(range(15))
-        self.out, self.into, self.own = [], [], own
+        h, q, e = BLK // 2, BLK // 4, BLK // 8
+        self.out, self.into = [], []
         right = here.device((here.x + 1) % 4, here.y, here.z, here.core)
         left = here.device((here.x + 3) % 4, here.y, here.z, here.core)
         across = here.device(here.x, 3 - here.y, here.z, here.core)
+        up = here.device(here.x, here.y, (here.z + 1) % 8, here.core)
+        down = here.device(here.x, here.y, (here.z + 7) % 8, here.core)
+        mate = here.mate()
         hi = here.y // 2
-
-        def rows(dx, flip, core, start=0, count=h):
+        p = (here.z % 2) * q
+        o = q - p
+
+        def rows(piece, core):
+            dx, flip, start, count = piece
             block = (1 - hi if flip else hi) * 4 + (here.x + dx) % 4
-            return feats.at[pl.ds(pl.multiple_of(block * BLK + core * h + start, h // 2), count), :]
-
-        def add(to, dx, flip, got_dx, got_flip, start=0, count=h, first=False):
-            i = next(n)
-            dst = rows(dx, flip, here.core, start, count)
-            src = own.at[pl.ds(pl.multiple_of(here.core * h, h), h), :] if first else dst
-            self.out.append(remote(src, dst, send.at[i], recv.at[i], to))
-            core = here.core if to is not mate else 1 - here.core
-            got = rows(got_dx, got_flip, core, start, count)
-            self.into.append(remote(got, got, send.at[i], recv.at[i], to))
-
-        mate = here.mate()
-        q = h // 2
-        add(right, 0, False, 3, False, first=True)
-        add(left, 0, False, 1, False, first=True)
-        add(across, 0, False, 0, True, first=True)
-        add(right, 3, False, 2, False, 0, q)
-        add(mate, 3, False, 3, False)
-        add(left, 1, False, 2, False, q, q)
-        add(mate, 1, False, 1, False)
-        add(right, 0, True, 3, True)
-        add(left, 0, True, 1, True)
-        add(mate, 0, True, 0, True)
-        add(across, 2, False, 2, True)
-        add(mate, 2, False, 2, False)
-        add(mate, 3, True, 3, True)
-        add(mate, 1, True, 1, True)
-        add(mate, 2, True, 2, True)
-
-    def run(self, steps):
+            return feats.at[pl.ds(pl.multiple_of(block * BLK + core * h + start, e), count), :]
+
+        def add(to, piece, got, source=None):
+            i = len(self.out)
+            dst = rows(piece, here.core)
+            self.out.append(remote(dst if source is None else source, dst, send.at[i], recv.at[i], to))
+            land = rows(got, 1 - here.core if to is mate else here.core)
+            self.into.append(remote(land, land, send.at[i], recv.at[i], to))
+
+        mine = own.at[pl.ds(pl.multiple_of(here.core * h + p, e), q), :]
+        N, F = False, True
+        add(right, (0, N, p, q), (3, N, p, q), mine)
+        add(left, (0, N, p, q), (1, N, p, q), mine)
+        add(across, (0, N, p, q), (0, F, p, q), mine)
+        add(right, (3, N, p, e), (2, N, p, e))
+        add(left, (1, N, p + e, e), (2, N, p + e, e))
+        add(right, (0, F, p, q), (3, F, p, q))
+        add(left, (0, F, p, q), (1, F, p, q))
+        add(up, (3, N, p, q), (3, N, o, q))
+        add(down, (1, N, p, q), (1, N, o, q))
+        add(up, (0, F, p, q), (0, F, o, q))
+        for piece in ((3, N, p, q), (1, N, p, q), (0, F, p, q)):
+            add(mate, piece, piece)
+        add(across, (2, N, p, q), (2, F, p, q))
+        add(down, (2, N, p, q), (2, N, o, q))
+        add(up, (3, F, p, q), (3, F, o, q))
+        add(down, (1, F, p, q), (1, F, o, q))
+        for piece in ((2, N, p, q), (3, F, p, q), (1, F, p, q)):
+            add(mate, piece, piece)
+        add(up, (2, F, p, e), (2, F, o, e))
+        add(down, (2, F, p + e, e), (2, F, o + e, e))
+        add(mate, (2, F, p, q), (2, F, p, q))
+        for piece in ((3, N, o, q), (1, N, o, q), (0, F, o, q)):
+            add(mate, piece, piece)
+        for piece in ((2, N, o, q), (3, F, o, q), (1, F, o, q), (2, F, o, q)):
+            add(mate, piece, piece)
+
+    def run(self, *steps):
         for got, go in steps:
             for i in got:
                 self.into[i].wait_recv()
@@ -118,16 +151,22 @@
                 self.out[i].start()
 
     def first(self):
-        self.run([((), (0, 1, 2))])
+        self.run(((), (0, 1, 2)))
 
     def second(self):
-        self.run([((0,), (3,)), ((1,), (5,)), ((2,), (7, 8)), ((), (4, 6, 9))])
+        self.run(((2,), (5, 6, 9)), ((0,), (3, 7)), ((1,), (4, 8)), ((), (10, 11, 12)))
 
     def third(self):
-        self.run([((3, 5), (10, 11)), ((7,), (12,)), ((8,), (13,))])
+        self.run(((3, 4), (13, 14)), ((5,), (15,)), ((6,), (16,)), ((), (17, 18, 19)))
 
     def fourth(self):
-        self.run([((10,), (14,)), ((4, 6, 9, 11, 12, 13, 14), ())])
+        self.run(((13,), (20, 21, 22)), ((7,), (23,)), ((8,), (24,)), ((9,), (25,)))
+
+    def fifth(self):
+        self.run(((14,), (26,)), ((15,), (27,)), ((16,), (28,)), ((20, 21), (29,)))
+
+    def sixth(self):
+        self.run(((10, 11, 12, 17, 18, 19, *range(22, 30)), ()))
 
     def finish(self):
         for c in self.out:
@@ -237,8 +276,8 @@
 
 
 def whole_kernel(
-    fanout, cnt_ref, og_hbm, pa_hbm, l2_hbm, hs_hbm, ci_hbm, hf_hbm, cf_hbm, one_hbm, two_hbm,
-    og, pa, l2, hs, ci, feats, rg, hp, c0, c1, two, sems, g_send, g_recv, one_bufs, one_sems, two_bufs, two_sems,
+    fanout, cnt_ref, og_hbm, pa_hbm, l2_hbm, hs_hbm, ci_hbm, hf_hbm, cf_hbm, one_ref, two_ref,
+    og, pa, l2, hs, ci, hu, cu, feats, rg, hp, c0, c1, acc, sems, g_send, g_recv, one_bufs, one_sems, two_bufs, two_sems,
 ):
     rows, dh = og.shape
     din = feats.shape[1]
@@ -270,7 +309,7 @@
     for c in copies[:3]:
         c.wait()
     count = cnt_ref[0]
-    two[...] = jnp.zeros_like(two)
+    acc[:dh, :] = jnp.zeros((dh, dh), jnp.float32)
 
     def some_rows(i, carry):
         at = pl.ds(pl.multiple_of(i * tile, tile), tile)
@@ -283,87 +322,96 @@
         )
         rg[at, :] = jnp.where(p > 0, back, 0.0).astype(jnp.bfloat16)
         activ = jnp.maximum(p, jnp.zeros_like(p))
-        two[...] += lax.dot_general(
+        acc[:dh, :] += lax.dot_general(
             activ, masked, (((0,), (0,)), ((), ())), preferred_element_type=jnp.float32
         )
         return carry
 
     lax.fori_loop(0, rows // tile, some_rows, 0)
-    sum_two.g[...] = two[...].reshape(dh // 8, 8, dh).astype(jnp.bfloat16)
+    sum_two.g[...] = acc[:dh, :].reshape(dh // 8, 8, dh).astype(jnp.bfloat16)
     sum_two.to_pair()
     for c in copies[3:5]:
         c.wait()
+    split_indices(ci, cu)
+    split_indices(hs, hu)
     n_hot = hot_n // BLK
 
-    def step(idx_ref, block, c_new, c_old, base):
-        if idx_ref is not None:
-            build_counts(idx_ref, block, c_new)
+    def step(refs, block, c_new, c_old, base):
+        if refs is not None:
+            build_counts(*refs, block, c_new)
         p = jnp.dot(c_old[...], rg[...], preferred_element_type=jnp.float32)
-        at = pl.ds(pl.multiple_of(base, BLK), BLK)
-        hp[at, :] = (p * (1.0 / fanout)).astype(jnp.bfloat16)
-
-    build_counts(ci, 0, c0)
-    step(ci, 1, c1, c0, hot_n)
+        size = BLK // 8
+        for b in range(8):
+            at = pl.ds(pl.multiple_of(base + b * size, size), size)
+            scaled = p[b * size : b * size + size] * (field_scale(b) / fanout)
+            hp[at, :] = scaled.astype(jnp.bfloat16)
+
+    cold, warm = (ci, cu), (hs, hu)
+    build_counts(*cold, 0, c0)
+    gather.second()
+    step(cold, 1, c1, c0, hot_n)
+    step(cold, 2, c0, c1, hot_n + BLK)
     sum_two.to_the_plane()
-    step(ci, 2, c0, c1, hot_n + BLK)
-    gather.second()
-    step(ci, 3, c1, c0, hot_n + 2 * BLK)
-    step(hs, 0, c0, c1, hot_n + 3 * BLK)
-    sum_two.to_the_column()
+    step(cold, 3, c1, c0, hot_n + 2 * BLK)
+    step(warm, 0, c0, c1, hot_n + 3 * BLK)
 
     def hot(i, carry):
-        step(hs, 2 * i + 1, c1, c0, 2 * i * BLK)
-        step(hs, 2 * i + 2, c0, c1, (2 * i + 1) * BLK)
+        step(warm, 2 * i + 1, c1, c0, 2 * i * BLK)
+        step(warm, 2 * i + 2, c0, c1, (2 * i + 1) * BLK)
 
         @pl.when(i == 0)
         def _():
-            sum_two.back_in_column()
+            gather.third()
 
         @pl.when(i == 1)
         def _():
-            gather.third()
-            sum_two.back_in_plane()
+            sum_two.to_the_column()
 
         @pl.when(i == 2)
         def _():
-            sum_two.back_to_pair()
+            gather.fourth()
+            sum_two.back_in_column()
 
         return carry
 
     lax.fori_loop(0, n_hot // 2 - 1, hot, 0)
-    step(hs, n_hot - 1, c1, c0, (n_hot - 2) * BLK)
+    step(warm, n_hot - 1, c1, c0, (n_hot - 2) * BLK)
     step(None, 0, c0, c1, (n_hot - 1) * BLK)
-    sum_two.received()
-    two_out = pltpu.make_async_copy(sum_two.out, two_hbm, sems.at[7])
-    two_out.start()
     for c in copies[5:]:
         c.wait()
-    gather.fourth()
+    gather.fifth()
+    sum_two.back_in_plane()
+    turned = (((0,), (0,)), ((), ()))
+    acc[...] = lax.dot_general(
+        feats[hot_n:, :], hp[hot_n:, :], turned, preferred_element_type=jnp.float32
+    )
+    gather.sixth()
 
     def some_sums(core):
-        at = pl.ds(pl.multiple_of(core * (din // 2), LANES), din // 2)
+        width, half = din // 2, sum_one.half
+        at = pl.ds(pl.multiple_of(core * width, LANES), width)
         sums = lax.dot_general(
-            feats[:, at], hp[...], (((0,), (0,)), ((), ())), preferred_element_type=jnp.float32
+            feats[:hot_n, at], hp[:hot_n, :], turned, preferred_element_type=jnp.float32
         )
-        half = sum_one.half
+        sums = sums + acc[at, :]
         sum_one.g[pl.ds(core * half, half)] = sums.reshape(half, 8, dh).astype(jnp.bfloat16)
 
     some_sums(1 - here.core)
     sum_one.to_pair()
     some_sums(here.core)
     sum_one.to_the_plane()
+    sum_two.back_to_pair()
     sum_one.to_the_column()
+    sum_two.received()
+    two_ref[...] = sum_two.out[...]
     sum_one.back_in_column()
     sum_one.back_in_plane()
     sum_one.back_to_pair()
     sum_one.received()
-    one_out = pltpu.make_async_copy(sum_one.out, one_hbm, sems.at[8])
-    one_out.start()
+    one_ref[...] = sum_one.out[...]
     gather.finish()
     sum_two.finish()
     sum_one.finish()
-    two_out.wait()
-    one_out.wait()
 
 
 def sum_scratch(rows, dh):
@@ -399,11 +447,13 @@
             jax.ShapeDtypeStruct((dh // 8, 8, dh), bf16),
         ),
         in_specs=[pl.BlockSpec(memory_space=pltpu.SMEM)] + [hbm] * 7,
-        out_specs=[hbm] * 2,
+        out_specs=[pl.BlockSpec(memory_space=vm)] * 2,
         scratch_shapes=[
             vm((rows, dh), bf16),
             vm((rows, dh), bf16),
             vm((dh, dh), bf16),
+            vm((hs.shape[1], rows), jnp.int32),
+            vm((ci.shape[1], rows), jnp.int32),
             vm((hs.shape[1], rows), jnp.int32),
             vm((ci.shape[1], rows), jnp.int32),
             vm((slots, din), bf16),
@@ -411,17 +461,17 @@
             vm((slots, dh), bf16),
             vm((BLK, rows), bf16),
             vm((BLK, rows), bf16),
-            vm((dh, dh), jnp.float32),
-            dma((9,)),
-            dma((15,)),
-            dma((15,)),
+            vm((din, dh), jnp.float32),
+            dma((7,)),
+            dma((30,)),
+            dma((30,)),
             one_bufs,
             one_sems,
             two_bufs,
             two_sems,
         ],
         compiler_params=pltpu.CompilerParams(
-            collective_id=0, has_side_effects=True, vmem_limit_bytes=56 << 20
+            collective_id=0, has_side_effects=True, vmem_limit_bytes=58 << 20
         ),
     )(cnt, og, pa, l2, hs.T, ci.T, hf, cf)
 

time: 87.7 us -> 80.7 us (0.920)
  Pallas kernels: 82.6 us -> 75.6 us
    pallas_call x1, Pallas kernels: 82.6 us -> 75.6 us  [whole_call(): pl.pallas_call(functools.partial(whole_kernel, fanout), out_shape=(jax.Sh...]
where the time goes in v3:
time: 80.7 us; the launch traced here: 80.6 us
  Pallas kernels  75.6 us (94%)
  other arithmetic  3.65 us (5%)
  between operations  1.3 us (2%)
    pallas_call x1, Pallas kernels, whole_call(): pl.pallas_call(functools.partial(whole_kernel, fanout), out_shape=(jax.Sh...  75.6 us
    convert_element_type x1, other arithmetic, on_device(): one.reshape(-1, dh).astype(jnp.float32)  2.55 us

profile of v3, /device:TPU:1, one launch (start us, length us, event | category | flops | bytes accessed | tf_op | source)
XLA Modules:
  0.0 80.6 jit_solution(10452974914296869282)
XLA Ops:
  1.3 75.6 %shard_map.95 = (bf16[96,8,512]{2,1,0:T(8,128)(2,1)}, bf16[64,8,512]{2,1,0:T(8,128)(2,1)}) custom-call(s32[1]{0:T(128)S(6)} %copy.10.cnt_ref, bf16[2048,512]{1,0:T(8,128)(2,1)} %og_hbm.1, bf16[2048,512]{1,0:T(8,128)(2,1)} %pa_hbm.1, bf16[512,512]{1,0:T(8,128)(2,1)} %l2_hbm.1, s32[10,2048]{1,0:T(8,128)} %bitcast.8, s32[15,2048]{1,0:T(8,128)} %bitcast.9, ...), custom_call_target="tpu_custom_call" | custom-call | tf_op jit(solution)/shard_map/pallas_call | solution.py:443
  76.9 0.0 copy-start
  76.9 2.5 %bitcast_convert_fusion = f32[768,512]{1,0:T(8,128)} fusion(bf16[96,8,512]{2,1,0:T(8,128)(2,1)} %get-tuple-element.4), kind=kLoop, calls=%fused_computation | loop fusion | flops 393216 | bytes 2359296 | tf_op jit(solution)/shard_map/convert_element_type | solution.py:487
  79.4 0.0 copy-done
  79.5 1.1 %bitcast_convert_fusion.1 = f32[512,512]{1,0:T(8,128)} fusion(bf16[64,8,512]{2,1,0:T(8,128)(2,1)S(1)} %copy-done), kind=kLoop, calls=%fused_computation.1 | loop fusion | flops 262144 | bytes 1572864 | tf_op jit(solution)/shard_map/convert_element_type | solution.py:487
Async XLA Ops:
  76.9 2.6 %copy-start = (bf16[64,8,512]{2,1,0:T(8,128)(2,1)S(1)}, bf16[64,8,512]{2,1,0:T(8,128)(2,1)}, u32[]{:S(2)}) copy-start(bf16[64,8,512]{2,1,0:T(8,128)(2,1)} %get-tuple-element.5) | copy-start | bytes 1572868

commit v4 on v3

--- a/solution.py
+++ b/solution.py
@@ -106,7 +106,7 @@
         def rows(piece, core):
             dx, flip, start, count = piece
             block = (1 - hi if flip else hi) * 4 + (here.x + dx) % 4
-            return feats.at[pl.ds(pl.multiple_of(block * BLK + core * h + start, e), count), :]
+            return feats.at[pl.ds(pl.multiple_of(block * BLK + core * h + start, 16), count), :]
 
         def add(to, piece, got, source=None):
             i = len(self.out)
@@ -129,7 +129,7 @@
         add(up, (0, F, p, q), (0, F, o, q))
         for piece in ((3, N, p, q), (1, N, p, q), (0, F, p, q)):
             add(mate, piece, piece)
-        add(across, (2, N, p, q), (2, F, p, q))
+        add(across, (2, N, p + 80, 48), (2, F, p + 80, 48))
         add(down, (2, N, p, q), (2, N, o, q))
         add(up, (3, F, p, q), (3, F, o, q))
         add(down, (1, F, p, q), (1, F, o, q))
@@ -142,6 +142,8 @@
             add(mate, piece, piece)
         for piece in ((2, N, o, q), (3, F, o, q), (1, F, o, q), (2, F, o, q)):
             add(mate, piece, piece)
+        add(right, (3, F, p, 48), (2, F, p, 48))
+        add(left, (1, F, p + 48, 32), (2, F, p + 48, 32))
 
     def run(self, *steps):
         for got, go in steps:
@@ -154,13 +156,16 @@
         self.run(((), (0, 1, 2)))
 
     def second(self):
-        self.run(((2,), (5, 6, 9)), ((0,), (3, 7)), ((1,), (4, 8)), ((), (10, 11, 12)))
+        self.run(((0,), (3,)), ((1,), (4,)), ((2,), (5, 6, 9, 7, 8)), ((), (10, 11, 12)))
 
     def third(self):
-        self.run(((3, 4), (13, 14)), ((5,), (15,)), ((6,), (16,)), ((), (17, 18, 19)))
+        self.run(((3, 4), (13, 14, 17)))
+
+    def third_across(self):
+        self.run(((5,), (30, 15)), ((6,), (31, 16)), ((), (18, 19)), ((7,), (23,)), ((8,), (24,)), ((9,), (25,)))
 
     def fourth(self):
-        self.run(((13,), (20, 21, 22)), ((7,), (23,)), ((8,), (24,)), ((9,), (25,)))
+        self.run(((13, 30, 31), (20, 21, 22)))
 
     def fifth(self):
         self.run(((14,), (26,)), ((15,), (27,)), ((16,), (28,)), ((20, 21), (29,)))
@@ -285,7 +290,7 @@
     hot_n = hf_hbm.shape[0] * 8
     here = Place()
     gather = Gather(here, hf_hbm, feats, g_send, g_recv)
-    sum_one = Sum(here, one_bufs, one_sems)
+    sums_one = [Sum(here, b, m) for b, m in zip(one_bufs, one_sems)]
     sum_two = Sum(here, two_bufs, two_sems)
     home = pl.ds(pl.multiple_of(lax.axis_index("clique") * BLK, BLK), BLK)
     pairs = [
@@ -348,10 +353,9 @@
 
     cold, warm = (ci, cu), (hs, hu)
     build_counts(*cold, 0, c0)
+    step(cold, 1, c1, c0, hot_n)
     gather.second()
-    step(cold, 1, c1, c0, hot_n)
     step(cold, 2, c0, c1, hot_n + BLK)
-    sum_two.to_the_plane()
     step(cold, 3, c1, c0, hot_n + 2 * BLK)
     step(warm, 0, c0, c1, hot_n + 3 * BLK)
 
@@ -365,53 +369,60 @@
 
         @pl.when(i == 1)
         def _():
-            sum_two.to_the_column()
-
-        @pl.when(i == 2)
-        def _():
-            gather.fourth()
-            sum_two.back_in_column()
+            gather.third_across()
 
         return carry
 
     lax.fori_loop(0, n_hot // 2 - 1, hot, 0)
     step(warm, n_hot - 1, c1, c0, (n_hot - 2) * BLK)
+    gather.fourth()
+    sum_two.to_the_plane()
     step(None, 0, c0, c1, (n_hot - 1) * BLK)
     for c in copies[5:]:
         c.wait()
-    gather.fifth()
-    sum_two.back_in_plane()
     turned = (((0,), (0,)), ((), ()))
     acc[...] = lax.dot_general(
         feats[hot_n:, :], hp[hot_n:, :], turned, preferred_element_type=jnp.float32
     )
+    gather.fifth()
     gather.sixth()
-
-    def some_sums(core):
-        width, half = din // 2, sum_one.half
-        at = pl.ds(pl.multiple_of(core * width, LANES), width)
-        sums = lax.dot_general(
+    width = din // len(sums_one)
+
+    def some_sums(n):
+        at = slice(n * width, n * width + width)
+        sums = acc[at, :] + lax.dot_general(
             feats[:hot_n, at], hp[:hot_n, :], turned, preferred_element_type=jnp.float32
         )
-        sums = sums + acc[at, :]
-        sum_one.g[pl.ds(core * half, half)] = sums.reshape(half, 8, dh).astype(jnp.bfloat16)
-
-    some_sums(1 - here.core)
-    sum_one.to_pair()
-    some_sums(here.core)
-    sum_one.to_the_plane()
+        sums_one[n].g[...] = sums.reshape(width // 8, 8, dh).astype(jnp.bfloat16)
+        sums_one[n].to_pair()
+
+    some_sums(0)
+    some_sums(1)
+    sums_one[0].to_the_plane()
+    sum_two.to_the_column()
+    some_sums(2)
+    sums_one[1].to_the_plane()
+    sums_one[2].to_the_plane()
+    sum_two.back_in_column()
+    for one in sums_one:
+        one.to_the_column()
+    sum_two.back_in_plane()
+    for one in sums_one:
+        one.back_in_column()
+    for one in sums_one:
+        one.back_in_plane()
     sum_two.back_to_pair()
-    sum_one.to_the_column()
     sum_two.received()
     two_ref[...] = sum_two.out[...]
-    sum_one.back_in_column()
-    sum_one.back_in_plane()
-    sum_one.back_to_pair()
-    sum_one.received()
-    one_ref[...] = sum_one.out[...]
+    for n, one in enumerate(sums_one):
+        one.back_to_pair()
+    for n, one in enumerate(sums_one):
+        one.received()
+        one_ref[n * width // 8 : (n + 1) * width // 8] = one.out[...]
     gather.finish()
     sum_two.finish()
-    sum_one.finish()
+    for one in sums_one:
+        one.finish()
 
 
 def sum_scratch(rows, dh):
@@ -438,7 +449,8 @@
     rows, dh = og.shape
     din = hf.shape[1]
     slots = hf.shape[0] * 8 + cf.shape[0]
-    one_bufs, one_sems = sum_scratch(din, dh)
+    chunks = [sum_scratch(din // 3, dh) for _ in range(3)]
+    one_bufs, one_sems = tuple(c[0] for c in chunks), tuple(c[1] for c in chunks)
     two_bufs, two_sems = sum_scratch(dh, dh)
     return pl.pallas_call(
         functools.partial(whole_kernel, fanout),
@@ -463,8 +475,8 @@
             vm((BLK, rows), bf16),
             vm((din, dh), jnp.float32),
             dma((7,)),
-            dma((30,)),
-            dma((30,)),
+            dma((32,)),
+            dma((32,)),
             one_bufs,
             one_sems,
             two_bufs,

time: 80.7 us -> 75.4 us (0.934)
  Pallas kernels: 75.6 us -> 70.4 us
    pallas_call x1, Pallas kernels: 75.6 us -> 70.4 us  [whole_call(): pl.pallas_call(functools.partial(whole_kernel, fanout), out_shape=(jax.Sh...]
where the time goes in v4:
time: 75.4 us; the launch traced here: 75.3 us
  Pallas kernels  70.4 us (93%)
  other arithmetic  3.65 us (5%)
  between operations  1.3 us (2%)
    pallas_call x1, Pallas kernels, whole_call(): pl.pallas_call(functools.partial(whole_kernel, fanout), out_shape=(jax.Sh...  70.4 us
    convert_element_type x1, other arithmetic, on_device(): one.reshape(-1, dh).astype(jnp.float32)  2.55 us

profile of v4, /device:TPU:1, one launch (start us, length us, event | category | flops | bytes accessed | tf_op | source)
XLA Modules:
  0.0 75.3 jit_solution(14130772997221005593)
XLA Ops:
  1.3 70.4 %shard_map.95 = (bf16[96,8,512]{2,1,0:T(8,128)(2,1)}, bf16[64,8,512]{2,1,0:T(8,128)(2,1)}) custom-call(s32[1]{0:T(128)S(6)} %copy.10.cnt_ref, bf16[2048,512]{1,0:T(8,128)(2,1)} %og_hbm.1, bf16[2048,512]{1,0:T(8,128)(2,1)} %pa_hbm.1, bf16[512,512]{1,0:T(8,128)(2,1)} %l2_hbm.1, s32[10,2048]{1,0:T(8,128)} %bitcast.8, s32[15,2048]{1,0:T(8,128)} %bitcast.9, ...), custom_call_target="tpu_custom_call" | custom-call | tf_op jit(solution)/shard_map/pallas_call | solution.py:455
  71.7 0.0 copy-start
  71.7 2.5 %bitcast_convert_fusion = f32[768,512]{1,0:T(8,128)} fusion(bf16[96,8,512]{2,1,0:T(8,128)(2,1)} %get-tuple-element.4), kind=kLoop, calls=%fused_computation | loop fusion | flops 393216 | bytes 2359296 | tf_op jit(solution)/shard_map/convert_element_type | solution.py:499
  74.2 0.0 copy-done
  74.2 1.1 %bitcast_convert_fusion.1 = f32[512,512]{1,0:T(8,128)} fusion(bf16[64,8,512]{2,1,0:T(8,128)(2,1)S(1)} %copy-done), kind=kLoop, calls=%fused_computation.1 | loop fusion | flops 262144 | bytes 1572864 | tf_op jit(solution)/shard_map/convert_element_type | solution.py:499
Async XLA Ops:
  71.7 2.6 %copy-start = (bf16[64,8,512]{2,1,0:T(8,128)(2,1)S(1)}, bf16[64,8,512]{2,1,0:T(8,128)(2,1)}, u32[]{:S(2)}) copy-start(bf16[64,8,512]{2,1,0:T(8,128)(2,1)} %get-tuple-element.5) | copy-start | bytes 1572868

commit v5 on v4

--- a/solution.py
+++ b/solution.py
@@ -182,7 +182,7 @@
     def __init__(self, here, bufs, sems):
         self.here = here
         self.g, self.rc, self.hs, self.ra, self.ms, self.rb, self.out = bufs
-        c_s, c_r, a_s, a_r, b_s, b_r, d_s, d_r, e_s, e_r, f_s, f_r = sems
+        c_s, c_r, a_s, a_r, b_s, b_r, e_s, e_r, f_s, f_r = sems
         g, rc, hs, ra, ms, rb, out = bufs
         half = rc.shape[0]
         per = half // 16
@@ -199,26 +199,9 @@
             remote(hs.at[pl.ds(q * per, per)], ra.at[q], a_s.at[q], a_r.at[q], d) for q, d in plane
         ]
 
-        def block(z):
-            return pl.ds(pl.multiple_of((z % 4) * LANES, LANES), LANES)
-
-        self.part = part = block(here.z)
-        self.to_column = [
-            remote(ms.at[:, :, block(z)], rb.at[here.z], b_s.at[z], b_r.at[here.z], d) for z, d in column
-        ]
-        self.of_column = [
-            remote(ms.at[:, :, part], rb.at[z], b_s.at[z], b_r.at[z], d) for z, d in column
-        ]
+        self.to_column = [remote(ms, rb.at[here.z], b_s.at[z], b_r.at[here.z], d) for z, d in column]
+        self.of_column = [remote(ms, rb.at[z], b_s.at[z], b_r.at[z], d) for z, d in column]
         self.slot = slot = pl.ds(self.mine + me * per, per)
-        steps = (1, 7, 6)
-        mine = out.at[slot, :, part]
-        self.back_to = [
-            remote(mine, mine, d_s.at[n], d_r.at[n], d) for n, (z, d) in enumerate(here.column(steps))
-        ]
-        self.back_of = []
-        for n, (z, d) in enumerate(here.column([8 - s for s in steps])):
-            theirs = out.at[slot, :, block(z)]
-            self.back_of.append(remote(theirs, theirs, d_s.at[n], d_r.at[n], d))
         self.home_to, self.home_of, self.pass_to, self.pass_of = [], [], [], []
         for q, d in plane:
             at = out.at[pl.ds(self.mine + q * per, per)]
@@ -248,19 +231,12 @@
         self.ms[...] = jnp.sum(self.ra[...].astype(jnp.float32), axis=0).astype(jnp.bfloat16)
         for c in self.to_column:
             c.start()
-        self.rb[self.here.z] = self.ms[:, :, self.part]
-
-    def back_in_column(self):
+        self.rb[self.here.z] = self.ms[...]
+
+    def back_in_plane(self):
         for c in self.of_column:
             c.wait_recv()
-        total = jnp.sum(self.rb[...].astype(jnp.float32), axis=0).astype(jnp.bfloat16)
-        self.out[self.slot, :, self.part] = total
-        for c in self.back_to:
-            c.start()
-
-    def back_in_plane(self):
-        for c in self.back_of:
-            c.wait_recv()
+        self.out[self.slot] = jnp.sum(self.rb[...].astype(jnp.float32), axis=0).astype(jnp.bfloat16)
         for c in self.home_to:
             c.start()
         self.own_to.start()
@@ -275,7 +251,7 @@
             c.wait_recv()
 
     def finish(self):
-        sent = [self.swap, *self.to_plane, *self.to_column, *self.back_to, *self.home_to, *self.pass_to]
+        sent = [self.swap, *self.to_plane, *self.to_column, *self.home_to, *self.pass_to]
         for c in [*sent, self.own_to]:
             c.wait_send()
 
@@ -403,19 +379,16 @@
     some_sums(2)
     sums_one[1].to_the_plane()
     sums_one[2].to_the_plane()
-    sum_two.back_in_column()
     for one in sums_one:
         one.to_the_column()
     sum_two.back_in_plane()
     for one in sums_one:
-        one.back_in_column()
-    for one in sums_one:
         one.back_in_plane()
     sum_two.back_to_pair()
+    for one in sums_one:
+        one.back_to_pair()
     sum_two.received()
     two_ref[...] = sum_two.out[...]
-    for n, one in enumerate(sums_one):
-        one.back_to_pair()
     for n, one in enumerate(sums_one):
         one.received()
         one_ref[n * width // 8 : (n + 1) * width // 8] = one.out[...]
@@ -435,10 +408,10 @@
         vm((half, 8, dh), bf16),
         vm((16, per, 8, dh), bf16),
         vm((per, 8, dh), bf16),
-        vm((8, per, 8, LANES), bf16),
+        vm((8, per, 8, dh), bf16),
         vm((units, 8, dh), bf16),
     )
-    sems = [dma, dma] + [dma((n,)) for n in (16, 16, 8, 8, 3, 3, 16, 16, 16, 16)]
+    sems = [dma, dma] + [dma((n,)) for n in (16, 16, 8, 8, 16, 16, 16, 16)]
     return bufs, tuple(sems)
 
 

time: 75.4 us -> 72.2 us (0.958)
  Pallas kernels: 70.4 us -> 67.2 us
    pallas_call x1, Pallas kernels: 70.4 us -> 67.2 us  [whole_call(): pl.pallas_call(functools.partial(whole_kernel, fanout), out_shape=(jax.Sh...]
where the time goes in v5:
time: 72.2 us; the launch traced here: 72.1 us
  Pallas kernels  67.2 us (93%)
  other arithmetic  3.65 us (5%)
  between operations  1.3 us (2%)
    pallas_call x1, Pallas kernels, whole_call(): pl.pallas_call(functools.partial(whole_kernel, fanout), out_shape=(jax.Sh...  67.2 us
    convert_element_type x1, other arithmetic, on_device(): one.reshape(-1, dh).astype(jnp.float32)  2.55 us

profile of v5, /device:TPU:1, one launch (start us, length us, event | category | flops | bytes accessed | tf_op | source)
XLA Modules:
  0.0 72.1 jit_solution(16262947268979856468)
XLA Ops:
  1.3 67.2 %shard_map.95 = (bf16[96,8,512]{2,1,0:T(8,128)(2,1)}, bf16[64,8,512]{2,1,0:T(8,128)(2,1)}) custom-call(s32[1]{0:T(128)S(6)} %copy.10.cnt_ref, bf16[2048,512]{1,0:T(8,128)(2,1)} %og_hbm.1, bf16[2048,512]{1,0:T(8,128)(2,1)} %pa_hbm.1, bf16[512,512]{1,0:T(8,128)(2,1)} %l2_hbm.1, s32[10,2048]{1,0:T(8,128)} %bitcast.8, s32[15,2048]{1,0:T(8,128)} %bitcast.9, ...), custom_call_target="tpu_custom_call" | custom-call | tf_op jit(solution)/shard_map/pallas_call | solution.py:428
  68.4 0.0 copy-start
  68.5 2.5 %bitcast_convert_fusion = f32[768,512]{1,0:T(8,128)} fusion(bf16[96,8,512]{2,1,0:T(8,128)(2,1)} %get-tuple-element.4), kind=kLoop, calls=%fused_computation | loop fusion | flops 393216 | bytes 2359296 | tf_op jit(solution)/shard_map/convert_element_type | solution.py:472
  71.0 0.0 copy-done
  71.0 1.1 %bitcast_convert_fusion.1 = f32[512,512]{1,0:T(8,128)} fusion(bf16[64,8,512]{2,1,0:T(8,128)(2,1)S(1)} %copy-done), kind=kLoop, calls=%fused_computation.1 | loop fusion | flops 262144 | bytes 1572864 | tf_op jit(solution)/shard_map/convert_element_type | solution.py:472
Async XLA Ops:
  68.4 2.6 %copy-start = (bf16[64,8,512]{2,1,0:T(8,128)(2,1)S(1)}, bf16[64,8,512]{2,1,0:T(8,128)(2,1)}, u32[]{:S(2)}) copy-start(bf16[64,8,512]{2,1,0:T(8,128)(2,1)} %get-tuple-element.5) | copy-start | bytes 1572868

commit v6 on v5

--- a/solution.py
+++ b/solution.py
@@ -19,12 +19,13 @@
     idx_ref[...] = (idx >> 9) * WB + (idx & (WB - 1))
 
 
-def build_counts(word_ref, unit_ref, block, c_ref):
+def build_counts(word_ref, unit_ref, block, c_ref, share=(0, 1)):
     k_n, rows = word_ref.shape
     assert k_n <= 15
     sub = lax.broadcasted_iota(jnp.int32, (8, LANES), 0) + block * WB
     low = jnp.full((8, LANES), 0x33333333, jnp.int32)
-    for j in range(rows // LANES):
+    part = rows // LANES // share[1]
+    for j in range(share[0] * part, share[0] * part + part):
         cols = slice(j * LANES, j * LANES + LANES)
         ws = [jnp.broadcast_to(word_ref[k : k + 1, cols], (8, LANES)) for k in range(k_n)]
         us = [jnp.broadcast_to(unit_ref[k : k + 1, cols], (8, LANES)) for k in range(k_n)]
@@ -258,7 +259,7 @@
 
 def whole_kernel(
     fanout, cnt_ref, og_hbm, pa_hbm, l2_hbm, hs_hbm, ci_hbm, hf_hbm, cf_hbm, one_ref, two_ref,
-    og, pa, l2, hs, ci, hu, cu, feats, rg, hp, c0, c1, acc, sems, g_send, g_recv, one_bufs, one_sems, two_bufs, two_sems,
+    og, pa, l2, hs, ci, hu, cu, feats, rg, hp, c0, c1, acc, sems, tile_sems, g_send, g_recv, one_bufs, one_sems, two_bufs, two_sems,
 ):
     rows, dh = og.shape
     din = feats.shape[1]
@@ -271,29 +272,34 @@
     home = pl.ds(pl.multiple_of(lax.axis_index("clique") * BLK, BLK), BLK)
     pairs = [
         (l2_hbm, l2),
-        (og_hbm, og),
-        (pa_hbm, pa),
         (ci_hbm, ci),
         (hs_hbm, hs),
         (cf_hbm, feats.at[pl.ds(hot_n, cf_hbm.shape[0]), :]),
         (hf_hbm, feats.at[home, :]),
     ]
     copies = [pltpu.make_async_copy(s, d, sems.at[i]) for i, (s, d) in enumerate(pairs)]
+    tiles = []
+    for i in range(rows // tile):
+        at = pl.ds(i * tile, tile)
+        for n, (s, d) in enumerate(((og_hbm, og), (pa_hbm, pa))):
+            tiles.append(pltpu.make_async_copy(s.at[at, :], d.at[at, :], tile_sems.at[2 * i + n]))
     barrier = pltpu.get_barrier_semaphore()
     peers = [here.mate()] + [d for _, d in here.plane()] + [d for _, d in here.column(range(1, 8))]
     for d in peers:
         pl.semaphore_signal(barrier, inc=1, device_id=d, device_id_type=MESH)
-    for c in copies:
+    for c in [copies[1], copies[0], *tiles, *copies[2:]]:
         c.start()
     pl.semaphore_wait(barrier, len(peers))
     gather.first()
-    for c in copies[:3]:
-        c.wait()
     count = cnt_ref[0]
     acc[:dh, :] = jnp.zeros((dh, dh), jnp.float32)
-
-    def some_rows(i, carry):
-        at = pl.ds(pl.multiple_of(i * tile, tile), tile)
+    copies[1].wait()
+    split_indices(ci, cu)
+    copies[0].wait()
+    for i in range(rows // tile):
+        tiles[2 * i].wait()
+        tiles[2 * i + 1].wait()
+        at = slice(i * tile, i * tile + tile)
         live = (lax.broadcasted_iota(jnp.int32, (tile, 1), 0) + i * tile) < count
         o = og[at, :]
         masked = jnp.where(live, o, jnp.zeros_like(o))
@@ -306,14 +312,10 @@
         acc[:dh, :] += lax.dot_general(
             activ, masked, (((0,), (0,)), ((), ())), preferred_element_type=jnp.float32
         )
-        return carry
-
-    lax.fori_loop(0, rows // tile, some_rows, 0)
+        build_counts(ci, cu, 0, c0, (i, rows // tile))
     sum_two.g[...] = acc[:dh, :].reshape(dh // 8, 8, dh).astype(jnp.bfloat16)
     sum_two.to_pair()
-    for c in copies[3:5]:
-        c.wait()
-    split_indices(ci, cu)
+    copies[2].wait()
     split_indices(hs, hu)
     n_hot = hot_n // BLK
 
@@ -328,7 +330,6 @@
             hp[at, :] = scaled.astype(jnp.bfloat16)
 
     cold, warm = (ci, cu), (hs, hu)
-    build_counts(*cold, 0, c0)
     step(cold, 1, c1, c0, hot_n)
     gather.second()
     step(cold, 2, c0, c1, hot_n + BLK)
@@ -354,7 +355,7 @@
     gather.fourth()
     sum_two.to_the_plane()
     step(None, 0, c0, c1, (n_hot - 1) * BLK)
-    for c in copies[5:]:
+    for c in copies[3:]:
         c.wait()
     turned = (((0,), (0,)), ((), ()))
     acc[...] = lax.dot_general(
@@ -362,6 +363,7 @@
     )
     gather.fifth()
     gather.sixth()
+    sum_two.to_the_column()
     width = din // len(sums_one)
 
     def some_sums(n):
@@ -375,13 +377,12 @@
     some_sums(0)
     some_sums(1)
     sums_one[0].to_the_plane()
-    sum_two.to_the_column()
     some_sums(2)
     sums_one[1].to_the_plane()
     sums_one[2].to_the_plane()
+    sum_two.back_in_plane()
     for one in sums_one:
         one.to_the_column()
-    sum_two.back_in_plane()
     for one in sums_one:
         one.back_in_plane()
     sum_two.back_to_pair()
@@ -447,7 +448,8 @@
             vm((BLK, rows), bf16),
             vm((BLK, rows), bf16),
             vm((din, dh), jnp.float32),
-            dma((7,)),
+            dma((5,)),
+            dma((2 * (rows // 512),)),
             dma((32,)),
             dma((32,)),
             one_bufs,

time: 72.2 us -> 73.2 us (1.014)
  Pallas kernels: 67.2 us -> 68.1 us
    pallas_call x1, Pallas kernels: 67.2 us -> 68.1 us  [whole_call(): pl.pallas_call(functools.partial(whole_kernel, fanout), out_shape=(jax.Sh...]
where the time goes in v6:
time: 73.2 us; the launch traced here: 73.1 us
  Pallas kernels  68.1 us (93%)
  other arithmetic  3.65 us (5%)
  between operations  1.3 us (2%)
    pallas_call x1, Pallas kernels, whole_call(): pl.pallas_call(functools.partial(whole_kernel, fanout), out_shape=(jax.Sh...  68.1 us
    convert_element_type x1, other arithmetic, on_device(): one.reshape(-1, dh).astype(jnp.float32)  2.55 us

profile of v6, /device:TPU:1, one launch (start us, length us, event | category | flops | bytes accessed | tf_op | source)
XLA Modules:
  0.0 73.1 jit_solution(2678888530175819290)
XLA Ops:
  1.3 68.1 %shard_map.95 = (bf16[96,8,512]{2,1,0:T(8,128)(2,1)}, bf16[64,8,512]{2,1,0:T(8,128)(2,1)}) custom-call(s32[1]{0:T(128)S(6)} %copy.10.cnt_ref, bf16[2048,512]{1,0:T(8,128)(2,1)} %og_hbm.1, bf16[2048,512]{1,0:T(8,128)(2,1)} %pa_hbm.1, bf16[512,512]{1,0:T(8,128)(2,1)} %l2_hbm.1, s32[10,2048]{1,0:T(8,128)} %bitcast.8, s32[15,2048]{1,0:T(8,128)} %bitcast.9, ...), custom_call_target="tpu_custom_call" | custom-call | tf_op jit(solution)/shard_map/pallas_call | solution.py:429
  69.4 0.0 copy-start
  69.4 2.5 %bitcast_convert_fusion = f32[768,512]{1,0:T(8,128)} fusion(bf16[96,8,512]{2,1,0:T(8,128)(2,1)} %get-tuple-element.4), kind=kLoop, calls=%fused_computation | loop fusion | flops 393216 | bytes 2359296 | tf_op jit(solution)/shard_map/convert_element_type | solution.py:474
  72.0 0.0 copy-done
  72.0 1.1 %bitcast_convert_fusion.1 = f32[512,512]{1,0:T(8,128)} fusion(bf16[64,8,512]{2,1,0:T(8,128)(2,1)S(1)} %copy-done), kind=kLoop, calls=%fused_computation.1 | loop fusion | flops 262144 | bytes 1572864 | tf_op jit(solution)/shard_map/convert_element_type | solution.py:474
Async XLA Ops:
  69.4 2.6 %copy-start = (bf16[64,8,512]{2,1,0:T(8,128)(2,1)S(1)}, bf16[64,8,512]{2,1,0:T(8,128)(2,1)}, u32[]{:S(2)}) copy-start(bf16[64,8,512]{2,1,0:T(8,128)(2,1)} %get-tuple-element.5) | copy-start | bytes 1572868

commit v7 on v6

--- a/solution.py
+++ b/solution.py
@@ -130,7 +130,7 @@
         add(up, (0, F, p, q), (0, F, o, q))
         for piece in ((3, N, p, q), (1, N, p, q), (0, F, p, q)):
             add(mate, piece, piece)
-        add(across, (2, N, p + 80, 48), (2, F, p + 80, 48))
+        add(across, (2, N, p + 32, 96), (2, F, p + 32, 96))
         add(down, (2, N, p, q), (2, N, o, q))
         add(up, (3, F, p, q), (3, F, o, q))
         add(down, (1, F, p, q), (1, F, o, q))
@@ -143,8 +143,8 @@
             add(mate, piece, piece)
         for piece in ((2, N, o, q), (3, F, o, q), (1, F, o, q), (2, F, o, q)):
             add(mate, piece, piece)
-        add(right, (3, F, p, 48), (2, F, p, 48))
-        add(left, (1, F, p + 48, 32), (2, F, p + 48, 32))
+        add(right, (3, F, p, 16), (2, F, p, 16))
+        add(left, (1, F, p + 16, 16), (2, F, p + 16, 16))
 
     def run(self, *steps):
         for got, go in steps:
@@ -351,8 +351,8 @@
         return carry
 
     lax.fori_loop(0, n_hot // 2 - 1, hot, 0)
+    gather.fourth()
     step(warm, n_hot - 1, c1, c0, (n_hot - 2) * BLK)
-    gather.fourth()
     sum_two.to_the_plane()
     step(None, 0, c0, c1, (n_hot - 1) * BLK)
     for c in copies[3:]:

time: 73.2 us -> 73.4 us (level)
  no operation moved by 1% of the time
where the time goes in v7:
time: 73.4 us; the launch traced here: 73.3 us
  Pallas kernels  68.4 us (93%)
  other arithmetic  3.65 us (5%)
  between operations  1.3 us (2%)
    pallas_call x1, Pallas kernels, whole_call(): pl.pallas_call(functools.partial(whole_kernel, fanout), out_shape=(jax.Sh...  68.4 us
    convert_element_type x1, other arithmetic, on_device(): one.reshape(-1, dh).astype(jnp.float32)  2.55 us

profile of v7, /device:TPU:1, one launch (start us, length us, event | category | flops | bytes accessed | tf_op | source)
XLA Modules:
  0.0 73.3 jit_solution(17056868981031081147)
XLA Ops:
  1.3 68.4 %shard_map.95 = (bf16[96,8,512]{2,1,0:T(8,128)(2,1)}, bf16[64,8,512]{2,1,0:T(8,128)(2,1)}) custom-call(s32[1]{0:T(128)S(6)} %copy.10.cnt_ref, bf16[2048,512]{1,0:T(8,128)(2,1)} %og_hbm.1, bf16[2048,512]{1,0:T(8,128)(2,1)} %pa_hbm.1, bf16[512,512]{1,0:T(8,128)(2,1)} %l2_hbm.1, s32[10,2048]{1,0:T(8,128)} %bitcast.8, s32[15,2048]{1,0:T(8,128)} %bitcast.9, ...), custom_call_target="tpu_custom_call" | custom-call | tf_op jit(solution)/shard_map/pallas_call | solution.py:429
  69.6 0.0 copy-start
  69.6 2.5 %bitcast_convert_fusion = f32[768,512]{1,0:T(8,128)} fusion(bf16[96,8,512]{2,1,0:T(8,128)(2,1)} %get-tuple-element.4), kind=kLoop, calls=%fused_computation | loop fusion | flops 393216 | bytes 2359296 | tf_op jit(solution)/shard_map/convert_element_type | solution.py:474
  72.2 0.0 copy-done
  72.2 1.1 %bitcast_convert_fusion.1 = f32[512,512]{1,0:T(8,128)} fusion(bf16[64,8,512]{2,1,0:T(8,128)(2,1)S(1)} %copy-done), kind=kLoop, calls=%fused_computation.1 | loop fusion | flops 262144 | bytes 1572864 | tf_op jit(solution)/shard_map/convert_element_type | solution.py:474
Async XLA Ops:
  69.6 2.6 %copy-start = (bf16[64,8,512]{2,1,0:T(8,128)(2,1)S(1)}, bf16[64,8,512]{2,1,0:T(8,128)(2,1)}, u32[]{:S(2)}) copy-start(bf16[64,8,512]{2,1,0:T(8,128)(2,1)} %get-tuple-element.5) | copy-start | bytes 1572868
